TPU v7x, 128 devices: a whole 4x4x4 slice. The times are simulated.
128 devices in a mesh: lat: 4 (over z_lo, core), lon: 32 (over y, x, z_hi).
Axes of the slice: x: 4, y: 4, z: 4 (z_hi: 2, z_lo: 2; z = z_hi * 2 + z_lo), core: 2. Of those that a mesh axis runs over, the one named last changes fastest.
Arguments:
- tracers: float32 [4, 32, 128, 4096], P(None, None, 'lat', 'lon'), may hold values from -6 to 6
- vel_east: float32 [32, 128, 4096], P(None, 'lat', 'lon'), may hold values from -0.18 to 0.18
- vel_north: float32 [32, 128, 4096], P(None, 'lat', 'lon'), may hold values from -0.18 to 0.18
- land_mask: int32 [32, 128, 4096], P(None, 'lat', 'lon'), may hold values 0 or 1
- step_area: float32 [128, 4096], P('lat', 'lon'), may hold values from 1.5 to 4
- float_cell: int32 [32768], P(('lat', 'lon')), may hold values from 0 to 4095
- float_owner: int32 [32768, 1], P(('lat', 'lon')), may hold values from 0 to 127; in each aligned block of 256 rows (0 to 255, 256 to 511, ...) at most 4 rows name the same one
Outputs:
- tracers_out: float32 [4, 32, 128, 4096], P(None, None, 'lat', 'lon')
- arrivals: float32 [65536, 128], P(('lat', 'lon'))
- arrival_counts: int32 [16384], P(('lat', 'lon'))
Inputs may be any that keep to these rules, and one draw needn't show every extreme that they name: `float_owner`: among the 256 rows of one device no device number appears more than 4 times, and in some device's rows one appears exactly 4 times.
All inputs are finite; a program needn't handle non-finite values. No bound on the sum of `land_mask` on one device may be relied on, other than what follows from the above.
Results may differ from a plain program's by a relative error of at most 0.0003.
Values sent between devices are 32-bit elements; how exact they have to be, the bound alone decides.
No kernel may reach another device: no remote copies, remote signals or barrier semaphores. Data moves between devices by JAX's collectives and lax.ppermute only.
A program may use at most 128 MiB of HBM per device.

v0:
```python
import jax
import jax.numpy as jnp
from jax import lax
from jax.experimental import pallas as pl
from jax.experimental.pallas import tpu as pltpu
from jax.sharding import PartitionSpec as P

CAP = 4
NT, LEV, ROWS, COLS = 4, 32, 32, 128
KG = LEV // 8
SLOTS = 24
S_VE, S_VN, S_M = 16, 18, 21
QUADS = 9
ABSENT = 1e30


def lanes():
    return lax.broadcasted_iota(jnp.int32, (8, COLS), 1)


def pick(x, index):
    return jnp.take_along_axis(x, index, axis=1, mode="promise_in_bounds")


def full(shape, dtype=jnp.float32):
    return jax.ShapeDtypeStruct(shape, dtype)


def params():
    return pltpu.CompilerParams(vmem_limit_bytes=56 * 1024 * 1024)


def vmem():
    return pl.BlockSpec(memory_space=pltpu.VMEM)


def rows_kernel(q_lo, q_hi, ve_lo, ve_hi, vn_lo, vn_hi, lm_lo, lm_hi, area, out_p, out_q):
    lat = lax.axis_index("lat")
    even = lat % 2 == 0
    fold = lat == 3
    flip = COLS - 1 - lanes()

    def take(ref, plane, row):
        return ref[pl.ds(plane * 8 + row, 8, stride=8), :]

    def mass(ref, kg, row, at):
        wet = take(ref, kg * 8, row).astype(jnp.float32)
        return wet * jnp.broadcast_to(area[at : at + 1, :], (8, COLS))

    for kg in range(KG):

        def put(slot, bottom, normal, mirrored):
            top = jnp.where(fold, pick(mirrored, flip), normal)
            out_p[slot, kg * 8 : kg * 8 + 8, :] = jnp.where(even, top, bottom)
            out_q[slot, kg * 8 : kg * 8 + 8, :] = jnp.where(even, bottom, top)

        for c in range(NT):
            plane = c * LEV + kg * 8
            low = [take(q_lo, plane, r) for r in range(4)]
            high = [take(q_hi, plane, 4 + r) for r in range(4)]
            for r in range(4):
                put(c * 4 + r, low[r], high[r], high[3 - r])
        low = [take(ve_lo, kg * 8, r) for r in range(2)]
        high = [take(ve_hi, kg * 8, 6 + r) for r in range(2)]
        for r in range(2):
            put(S_VE + r, low[r], high[r], -high[1 - r])
        low = [take(vn_lo, kg * 8, r) for r in (0, 0, 1)]
        high = [take(vn_hi, kg * 8, 5 + r) for r in range(3)]
        for r in range(3):
            put(S_VN + r, low[r], high[r], -high[2 - r])
        low = [mass(lm_lo, kg, r, r) for r in range(3)]
        high = [mass(lm_hi, kg, 5 + r, 29 + r) for r in range(3)]
        for r in range(3):
            put(S_M + r, low[r], high[r], high[2 - r])


def pack_rows(tracers, ve, vn, lm, area):
    def edge(array, last):
        n = array.shape[0]
        block = array.reshape(n, ROWS // 8, 8, COLS)[:, 3 if last else 0]
        return block.reshape(n * 8, COLS)

    def spec(n, at):
        return pl.BlockSpec((n, 8, COLS), lambda i: (0, at, 0))

    def body(*refs):
        refs = list(refs)
        flat = [r.reshape(r.shape[0] * 8, COLS) for r in refs[:8]]
        rows_kernel(*flat, *refs[8:])

    q3 = tracers.reshape(NT * LEV, ROWS, COLS)
    return pl.pallas_call(
        body,
        grid=(1,),
        in_specs=[
            spec(NT * LEV, 0), spec(NT * LEV, 3), spec(LEV, 0), spec(LEV, 3),
            spec(LEV, 0), spec(LEV, 3), spec(LEV, 0), spec(LEV, 3),
            pl.BlockSpec((ROWS, COLS), lambda i: (0, 0)),
        ],
        out_specs=[pl.BlockSpec((SLOTS, LEV, COLS), lambda i: (0, 0, 0))] * 2,
        out_shape=[full((SLOTS, LEV, COLS))] * 2,
        compiler_params=params(),
        name="pack_rows",
    )(q3, q3, ve, ve, vn, vn, lm, lm, area)


class Band:
    def __init__(self, q, ve, vn, lm, area, in_p, in_q):
        self.q, self.ve, self.vn, self.lm, self.area = q, ve, vn, lm, area
        self.in_p, self.in_q = in_p, in_q
        self.even = lax.axis_index("lat") % 2 == 0

    def ghost(self, north, slot, kg):
        a = self.in_p[slot, kg * 8 : kg * 8 + 8, :]
        b = self.in_q[slot, kg * 8 : kg * 8 + 8, :]
        return jnp.where(self.even, a, b) if north else jnp.where(self.even, b, a)

    def own(self, ref, plane, row):
        return ref[pl.ds(plane * ROWS + row, 8, stride=ROWS), :]

    def tracer(self, c, kg, row):
        if row < 0:
            return self.ghost(False, c * 4 + row + 4, kg)
        if row >= ROWS:
            return self.ghost(True, c * 4 + row - ROWS, kg)
        return self.own(self.q, c * LEV + kg * 8, row)

    def east(self, kg, row):
        if row < 0:
            return self.ghost(False, S_VE + row + 2, kg)
        if row >= ROWS:
            return self.ghost(True, S_VE + row - ROWS, kg)
        return self.own(self.ve, kg * 8, row)

    def north(self, kg, face):
        if face < 0:
            return self.ghost(False, S_VN + face + 3, kg)
        if face >= ROWS:
            return self.ghost(True, S_VN + 1 + face - ROWS, kg)
        return self.own(self.vn, kg * 8, face)

    def mass(self, kg, row):
        if row < 0:
            return self.ghost(False, S_M + row + 3, kg)
        if row >= ROWS:
            return self.ghost(True, S_M + row - ROWS, kg)
        wet = self.own(self.lm, kg * 8, row).astype(jnp.float32)
        return wet * jnp.broadcast_to(self.area[row : row + 1, :], (8, COLS))

    def fields(self, kg, row):
        return [self.tracer(c, kg, row) for c in range(NT)] + [
            self.east(kg, row), self.north(kg, row), self.mass(kg, row)
        ]


def quad_rows(quad):
    return [-2, -1, ROWS, ROWS + 1] if quad == QUADS - 1 else [quad * 4 + r for r in range(4)]


def cols_kernel(q, ve, vn, lm, area, in_p, in_q, out_r, out_s):
    band = Band(q, ve, vn, lm, area, in_p, in_q)
    even = lax.axis_index("lon") % 2 == 0
    lane = lanes()
    ends = jnp.where(lane < 64, lane % 4, COLS - 4 + lane % 4)
    place = (lane % 64) // 4
    for quad in range(QUADS):
        for kg in range(KG):
            halves = []
            for pair in range(2):
                acc = jnp.zeros((8, COLS), jnp.float32)
                for h in range(2):
                    for f, x in enumerate(band.fields(kg, quad_rows(quad)[pair * 2 + h])):
                        acc = jnp.where(place == 8 * h + f, pick(x, ends), acc)
                halves.append(acc)
            west = jnp.where(lane < 64, halves[0], pltpu.roll(halves[1], 64, 1))
            east = jnp.where(lane < 64, pltpu.roll(halves[0], 64, 1), halves[1])
            out_r[quad, kg * 8 : kg * 8 + 8, :] = jnp.where(even, east, west)
            out_s[quad, kg * 8 : kg * 8 + 8, :] = jnp.where(even, west, east)


def pack_cols(q, ve, vn, lm, area, in_p, in_q):
    return pl.pallas_call(
        cols_kernel,
        out_shape=[full((QUADS, LEV, COLS))] * 2,
        compiler_params=params(),
        name="pack_cols",
    )(q, ve, vn, lm, area, in_p, in_q)


ROW_LO, ROW_HI = -4, 36
SIXTH = 1.0 / 6.0


def along_columns(e, w):
    right = pltpu.roll(e, COLS - 1, 1)
    triple = 3.0 * e
    both = e + right
    behind = triple - pltpu.roll(e, 1, 1)
    ahead = pltpu.roll(triple - right, COLS - 1, 1)
    flux = w * (both + both + jnp.where(w > 0, behind, ahead))
    return flux - pltpu.roll(flux, 1, 1)


def along_rows(a, b, c, d, w):
    both = b + c
    return w * (both + both + jnp.where(w > 0, 3.0 * b - a, 3.0 * c - d))


def advance_kernel(q, ve, vn, lm, area, in_p, in_q, in_r, in_s, cell, slot, out, outbox,
                   qs, se, sn, sm, done, flat):
    band = Band(q, ve, vn, lm, area, in_p, in_q)
    lat = lax.axis_index("lat")
    fold = lat == 3
    even = lax.axis_index("lon") % 2 == 0
    lane = lanes()
    spot = lane % 32
    group = lane // 32
    own_cols = jnp.where((spot >= 4) & (spot < 12), spot - 4, jnp.where((spot >= 12) & (spot < 20), spot + 108, 0))
    low_halo = spot < 4
    high_halo = (spot >= 20) & (spot < 24)
    halo_at = jnp.where(low_halo, spot, jnp.where(high_halo, spot - 20, 0))

    def strip_of_tracers(parts):
        x = [pick(p, own_cols) for p in parts]
        return jnp.where(group < 2, jnp.where(group == 0, x[0], x[1]), jnp.where(group == 2, x[2], x[3]))

    def with_halo(x, west, east, index):
        return jnp.where(low_halo, pick(west, index), jnp.where(high_halo, pick(east, index), x))

    for kg in range(KG):
        ks = slice(kg * 8, kg * 8 + 8)
        raw = {}
        for row in range(ROW_LO, ROW_HI):
            parts = [band.tracer(c, kg, row) for c in range(NT)]
            for c in range(NT):
                qs[c, row - ROW_LO, ks, :] = parts[c]
            strip = strip_of_tracers(parts)
            main = {}
            edge = {}
            if -2 <= row < ROWS + 2:
                main["e"] = band.east(kg, row)
            if -3 <= row < ROWS + 2:
                main["n"] = band.north(kg, row)
            if -3 <= row < ROWS + 3:
                main["m"] = band.mass(kg, row)
            for name, x in main.items():
                edge[name] = pick(x, own_cols)
            if -2 <= row < ROWS + 2:
                if 0 <= row < ROWS:
                    quad, rq = row // 4, row % 4
                else:
                    quad, rq = QUADS - 1, (row + 2 if row < 0 else row - ROWS + 2)
                r_in = in_r[quad, ks, :]
                s_in = in_s[quad, ks, :]
                west = jnp.where(even, s_in, r_in)
                east = jnp.where(even, r_in, s_in)
                strip = with_halo(strip, west, east, 32 * rq + 4 * group + halo_at)
                for f, name in ((4, "e"), (5, "n"), (6, "m")):
                    edge[name] = with_halo(edge[name], west, east, 32 * rq + 4 * f + halo_at)
            qs[NT, row - ROW_LO, ks, :] = strip
            raw[row] = (main, edge)
        for part in range(2):
            for row in range(-2, ROWS + 2):
                f = raw[row][part]
                v = f["e"]
                if row >= ROWS:
                    v = jnp.where(fold, pltpu.roll(v, COLS - 1, 1), v)
                open_to = jnp.minimum(f["m"], pltpu.roll(f["m"], COLS - 1, 1)) > 0
                se[part, row + 2, ks, :] = jnp.where(open_to, v * SIXTH, 0.0)
                sm[part, row + 2, ks, :] = f["m"]
            for face in range(-3, ROWS + 2):
                v = raw[face][part]["n"]
                open_to = jnp.minimum(raw[face][part]["m"], raw[face + 1][part]["m"]) > 0
                sn[part, face + 3, ks, :] = jnp.where(open_to, v * SIXTH, 0.0)
                if face == ROWS - 1:
                    other = band.ghost(True, S_VN, kg)
                    if part == 1:
                        other = pick(other, own_cols)
                    other = jnp.where(fold, other, v)
                    sn[part, ROWS + 5, ks, :] = jnp.where(open_to, other * SIXTH, 0.0)

    def column(step, _):
        t = step // KG
        base = pl.multiple_of((step % KG) * 8, 8)
        ks = pl.ds(base, 8)
        s = t // NT
        first = {}
        e = {}
        load = lambda row: qs[t, row - ROW_LO, ks, :]
        for row in range(-4, 0):
            e[row] = load(row)
        below = None
        prev = None

        def finish(row, prev_flux):
            upper = along_rows(first[row - 1], first[row], first[row + 1], first[row + 2], sn[s, row + 3, ks, :])
            if prev_flux is None:
                prev_flux = along_rows(first[row - 2], first[row - 1], first[row], first[row + 1], sn[s, row + 2, ks, :])
            change = along_columns(first[row], se[s, row + 2, ks, :]) + (upper - prev_flux)
            done[t, row, ks, :] = first[row] - sm[s, row + 2, ks, :] * change
            return upper

        for row in range(-2, ROWS + 2):
            e[row + 2] = load(row + 2)
            if below is None:
                below = along_rows(e[row - 2], e[row - 1], e[row], e[row + 1], sn[s, row + 2, ks, :])
            if row == ROWS:
                below = along_rows(e[row - 2], e[row - 1], e[row], e[row + 1], sn[s, ROWS + 5, ks, :])
            above = along_rows(e[row - 1], e[row], e[row + 1], e[row + 2], sn[s, row + 3, ks, :])
            change = along_columns(e[row], se[s, row + 2, ks, :]) + (above - below)
            first[row] = e[row] - sm[s, row + 2, ks, :] * change
            below = above
            if row - 2 >= 0:
                prev = finish(row - 2, prev)
        return 0

    lax.fori_loop(0, (NT + 1) * KG, column, 0)

    edge_cols = (lane < 4) | (lane >= COLS - 4)
    edge_at = jnp.where(lane < 4, lane + 4, jnp.where(lane >= COLS - 4, lane - (COLS - 4) + 16, 0))

    def merge(row, _):
        planes = []
        for c in range(NT):
            for kg in range(KG):
                ks = slice(kg * 8, kg * 8 + 8)
                x = jnp.where(edge_cols, pick(done[NT, row, ks, :], edge_at + 32 * c), done[c, row, ks, :])
                out[pl.ds((c * LEV + kg * 8) * ROWS + row, 8, stride=ROWS), :] = x
                planes.append(x)
        flat[pl.ds(pl.multiple_of(row * COLS, COLS), COLS), :] = jnp.concatenate(planes, axis=0).T
        return 0

    lax.fori_loop(0, ROWS, merge, 0)

    mark = jnp.where(lane == 0, ABSENT, 0.0)
    for i in range(outbox.shape[0] // 8):
        outbox[i * 8 : i * 8 + 8, :] = mark

    def send(i, _):
        for j in range(8):
            outbox[pl.ds(slot[i * 8 + j], 1), :] = flat[pl.ds(cell[i * 8 + j], 1), :]
        return 0

    lax.fori_loop(0, cell.shape[0] // 8, send, 0)


def both_steps(q, ve, vn, lm, area, in_p, in_q, in_r, in_s, cell, slot, devices):
    smem = pl.BlockSpec(memory_space=pltpu.SMEM)
    return pl.pallas_call(
        advance_kernel,
        in_specs=[vmem()] * 9 + [smem, smem],
        out_specs=[vmem()] * 2,
        out_shape=[full(q.shape), full((devices * CAP, NT * LEV))],
        scratch_shapes=[
            pltpu.VMEM((NT + 1, ROW_HI - ROW_LO, LEV, COLS), jnp.float32),
            pltpu.VMEM((2, ROWS + 4, LEV, COLS), jnp.float32),
            pltpu.VMEM((2, ROWS + 6, LEV, COLS), jnp.float32),
            pltpu.VMEM((2, ROWS + 4, LEV, COLS), jnp.float32),
            pltpu.VMEM((NT + 1, ROWS, LEV, COLS), jnp.float32),
            pltpu.VMEM((ROWS * COLS, NT * LEV), jnp.float32),
        ],
        compiler_params=params(),
        name="both_steps",
    )(q, ve, vn, lm, area, in_p, in_q, in_r, in_s, cell, slot)


def slots_kernel(column, row, out):
    n = row.shape[1]
    at = lax.broadcasted_iota(jnp.int32, (n, n), 0)
    me = lax.broadcasted_iota(jnp.int32, (n, n), 1)
    same = (jnp.broadcast_to(column[...], (n, n)) == jnp.broadcast_to(row[...], (n, n))) & (at < me)
    rank = jnp.sum(jnp.where(same, 1.0, 0.0), axis=0, keepdims=True).astype(jnp.int32)
    out[...] = row[...] * CAP + rank


def float_slots(owner):
    n = owner.shape[0]
    return pl.pallas_call(
        slots_kernel, out_shape=full((1, n), jnp.int32), compiler_params=params(), name="float_slots"
    )(owner, owner.reshape(1, n)).reshape(n)


def arrivals_kernel(inbox, out, counts):
    total = jnp.zeros((8, COLS), jnp.float32)
    sub = lax.broadcasted_iota(jnp.int32, (8, COLS), 0)
    lane = lanes()
    for i in range(inbox.shape[0] // 8):
        x = inbox[i * 8 : i * 8 + 8, :]
        here = jnp.broadcast_to(x[:, 0:1], (8, COLS)) < ABSENT * 0.5
        out[i * 8 : i * 8 + 8, :] = jnp.where(here, x, 0.0)
        total = total + jnp.where(here & (lane == (i * 8 + sub) // CAP), 1.0, 0.0)
    counts[...] = jnp.sum(total, axis=0, keepdims=True).astype(jnp.int32)


def unpack_arrivals(inbox):
    n = inbox.shape[0]
    return pl.pallas_call(
        arrivals_kernel,
        out_shape=[full(inbox.shape), full((1, n // CAP), jnp.int32)],
        compiler_params=params(),
        name="unpack_arrivals",
    )(inbox)


def local(tracers, vel_east, vel_north, land_mask, step_area, float_cell, float_owner):
    lat_n, lon_n = lax.axis_size("lat"), lax.axis_size("lon")
    axes = ("lat", "lon")

    def swap(target):
        pairs = []
        for b in range(lat_n):
            for l in range(lon_n):
                to = target(b, l)
                if to is not None:
                    pairs.append((b * lon_n + l, to[0] * lon_n + to[1]))
        return lambda x: lax.ppermute(x, axes, pairs)

    swap_p = swap(lambda b, l: (b ^ 1, l))
    swap_q = swap(lambda b, l: {1: (2, l), 2: (1, l), 3: (3, lon_n - 1 - l)}.get(b))
    swap_r = swap(lambda b, l: (b, l ^ 1))
    swap_s = swap(lambda b, l: (b, (((l + 1) ^ 1) - 1) % lon_n))

    q = tracers.reshape(NT * LEV * ROWS, COLS)
    ve = vel_east.reshape(LEV * ROWS, COLS)
    vn = vel_north.reshape(LEV * ROWS, COLS)
    lm = land_mask.reshape(LEV * ROWS, COLS)
    slot = float_slots(float_owner)
    out_p, out_q = pack_rows(tracers, vel_east, vel_north, land_mask, step_area)
    in_q = swap_q(out_q)
    in_p = swap_p(out_p)
    out_r, out_s = pack_cols(q, ve, vn, lm, step_area, in_p, in_q)
    in_s = swap_s(out_s)
    in_r = swap_r(out_r)
    out, outbox = both_steps(q, ve, vn, lm, step_area, in_p, in_q, in_r, in_s, float_cell, slot, lat_n * lon_n)
    inbox = lax.all_to_all(
        outbox.reshape(lat_n * lon_n, CAP, NT * LEV), axes, split_axis=0, concat_axis=0, tiled=True
    ).reshape(lat_n * lon_n * CAP, NT * LEV)
    arrivals, counts = unpack_arrivals(inbox)
    return out.reshape(tracers.shape), arrivals, counts.reshape(-1)


def solution(mesh):
    placed = (
        P(None, None, "lat", "lon"),
        P(None, "lat", "lon"),
        P(None, "lat", "lon"),
        P(None, "lat", "lon"),
        P("lat", "lon"),
        P(("lat", "lon")),
        P(("lat", "lon"), None),
    )
    return jax.shard_map(
        local,
        mesh=mesh,
        in_specs=placed,
        out_specs=(P(None, None, "lat", "lon"), P(("lat", "lon"), None), P(("lat", "lon"))),
        check_vma=False,
    )
```

profile of v0, /device:TPU:1, one launch (start us, length us, event | category | flops | bytes accessed | tf_op | source)
XLA Modules:
  0.0 86.7 jit_solution(5998440388790296746)
XLA Ops:
  0.6 2.5 %pack_rows.1 = (f32[24,32,128]{2,1,0:T(8,128)}, f32[24,32,128]{2,1,0:T(8,128)}) custom-call(f32[128,32,128]{2,1,0:T(8,128)} %bitcast.11, f32[128,32,128]{2,1,0:T(8,128)} %bitcast.12, f32[32,32,128]{2,1,0:T(8,128)} %refs_3_.1, f32[32,32,128]{2,1,0:T(8,128)} %refs_3_.1, f32[32,32,128]{2,1,0:T(8,128)} %refs_5_.1, f32[32,32,128]{2,1,0:T(8,128)} %refs_5_.1, ...), custom_call_target="tpu_custom_call" | custom-call | tf_op jit(solution)/shard_map/pack_rows/pallas_call | solution.py:92
  3.2 1.4 %collective-permute-start = (f32[24,32,128]{2,1,0:T(8,128)}, f32[24,32,128]{2,1,0:T(8,128)S(1)}, u32[]{:S(2)}, u32[]{:S(2)}) collective-permute-start(f32[24,32,128]{2,1,0:T(8,128)} %get-tuple-element.11), channel_id=1, source_target_pairs={{0,32},{1,33},{2,34},{3,35},{4,36},{5,37},{6,38},{7,39},{8,40},{9,... | collective-permute-start | bytes 1179656 | tf_op jit(solution)/shard_map/ppermute | solution.py:416
  4.5 3.5 %collective-permute-start.1 = (f32[24,32,128]{2,1,0:T(8,128)}, f32[24,32,128]{2,1,0:T(8,128)S(1)}, u32[]{:S(2)}, u32[]{:S(2)}) collective-permute-start(f32[24,32,128]{2,1,0:T(8,128)} %get-tuple-element.12), channel_id=1, source_target_pairs={{32,64},{33,65},{34,66},{35,67},{36,68},{37,69},{38,70},{39,71},{4... | collective-permute-start | bytes 1179656 | tf_op jit(solution)/shard_map/ppermute | solution.py:416
  8.1 0.0 collective-permute-done.in_p
  8.1 0.0 copy-start
  8.1 5.7 %collective-permute-done.1.in_q = f32[24,32,128]{2,1,0:T(8,128)S(1)} collective-permute-done((f32[24,32,128]{2,1,0:T(8,128)}, f32[24,32,128]{2,1,0:T(8,128)S(1)}, u32[]{:S(2)}, u32[]{:S(2)}) %collective-permute-start.1) | collective-permute-done | bytes 393248 | tf_op jit(solution)/shard_map/ppermute | solution.py:416
  13.8 0.0 copy-start.1
  13.8 0.0 copy-done
  13.8 0.7 copy-done.1
  14.6 0.0 copy-start.4
  14.6 6.5 %pack_cols.1 = (f32[9,32,128]{2,1,0:T(8,128)}, f32[9,32,128]{2,1,0:T(8,128)}) custom-call(f32[4096,128]{1,0:T(8,128)} %bitcast.13, f32[1024,128]{1,0:T(8,128)} %bitcast.15, f32[1024,128]{1,0:T(8,128)} %bitcast.17, s32[1024,128]{1,0:T(8,128)} %bitcast.19, f32[32,128]{1,0:T(8,128)} %area.3, f32[24,32,128]{2,1,0:T(8,128)} %copy-done, f32[24,32,128]{2,1,0:T(8,128)} %copy-done.1), custom_call_target="tpu_custom_call" | custom-call | tf_op jit(solution)/shard_map/pack_cols/pallas_call | solution.py:182
  21.1 7.9 %collective-permute-start.2 = (f32[9,32,128]{2,1,0:T(8,128)}, f32[9,32,128]{2,1,0:T(8,128)S(1)}, u32[]{:S(2)}, u32[]{:S(2)}) collective-permute-start(f32[9,32,128]{2,1,0:T(8,128)} %get-tuple-element.13), channel_id=1, source_target_pairs={{0,1},{1,0},{2,3},{3,2},{4,5},{5,4},{6,7},{7,6},{8,9},{9,8},{10,11... | collective-permute-start | bytes 442376 | tf_op jit(solution)/shard_map/ppermute | solution.py:416
  29.0 4.6 %collective-permute-start.3 = (f32[9,32,128]{2,1,0:T(8,128)}, f32[9,32,128]{2,1,0:T(8,128)S(1)}, u32[]{:S(2)}, u32[]{:S(2)}) collective-permute-start(f32[9,32,128]{2,1,0:T(8,128)} %get-tuple-element.14), channel_id=1, source_target_pairs={{0,31},{1,2},{2,1},{3,4},{4,3},{5,6},{6,5},{7,8},{8,7},{9,10},{10,... | collective-permute-start | bytes 442376 | tf_op jit(solution)/shard_map/ppermute | solution.py:416
  33.6 0.0 copy-done.4
  33.6 0.8 copy.10.column
  34.4 1.6 %float_slots.1 = s32[1,256]{1,0:T(1,128)} custom-call(s32[256,1]{1,0:T(8,128)} %copy.10.column, s32[1,256]{1,0:T(1,128)} %bitcast.23), custom_call_target="tpu_custom_call" | custom-call | tf_op jit(solution)/shard_map/float_slots/pallas_call | solution.py:378
  36.1 0.0 collective-permute-done.2.in_r
  36.1 0.0 copy-start.2
  36.1 2.9 %collective-permute-done.3.in_s = f32[9,32,128]{2,1,0:T(8,128)S(1)} collective-permute-done((f32[9,32,128]{2,1,0:T(8,128)}, f32[9,32,128]{2,1,0:T(8,128)S(1)}, u32[]{:S(2)}, u32[]{:S(2)}) %collective-permute-start.3) | collective-permute-done | bytes 147488 | tf_op jit(solution)/shard_map/ppermute | solution.py:416
  38.9 0.0 copy-start.3
  38.9 0.0 copy-done.2
  38.9 0.7 copy-done.3
  39.6 26.7 %both_steps.1 = (f32[4096,128]{1,0:T(8,128)}, f32[512,128]{1,0:T(8,128)}) custom-call(f32[4096,128]{1,0:T(8,128)} %bitcast.14, f32[1024,128]{1,0:T(8,128)} %bitcast.16, f32[1024,128]{1,0:T(8,128)} %bitcast.18, s32[1024,128]{1,0:T(8,128)} %bitcast.20, f32[32,128]{1,0:T(8,128)} %area.3, f32[24,32,128]{2,1,0:T(8,128)} %copy-done, f32[24,32,128]{2,1,0:T(8,128)} %copy-done.1, ...), custom_call_target="tpu_custom_call" | custom-call | tf_op jit(solution)/shard_map/both_steps/pallas_call | solution.py:349
  66.3 18.6 %all_to_all.5 = f32[128,4,128]{2,1,0:T(4,128)} all-to-all(f32[128,4,128]{2,1,0:T(4,128)} %bitcast.22), channel_id=1, replica_groups=mesh['lat'=4,'lon'=32] {'lat','lon'}, dimensions={0} | all-to-all | bytes 524288 | tf_op jit(solution)/shard_map/all_to_all | solution.py:435
  84.9 1.8 %unpack_arrivals.1 = (f32[512,128]{1,0:T(8,128)}, s32[1,128]{1,0:T(1,128)}) custom-call(f32[512,128]{1,0:T(8,128)} %bitcast.21), custom_call_target="tpu_custom_call" | custom-call | tf_op jit(solution)/shard_map/unpack_arrivals/pallas_call | solution.py:397
Async XLA Ops:
  3.2 4.9 %collective-permute-start = (f32[24,32,128]{2,1,0:T(8,128)}, f32[24,32,128]{2,1,0:T(8,128)S(1)}, u32[]{:S(2)}, u32[]{:S(2)}) collective-permute-start(f32[24,32,128]{2,1,0:T(8,128)} %get-tuple-element.11), channel_id=1, source_target_pairs={{0,32},{1,33},{2,34},{3,35},{4,36},{5,37},{6,38},{7,39},{8,40},{9,... | collective-permute-start | bytes 1179656 | tf_op jit(solution)/shard_map/ppermute | solution.py:416
  4.5 9.3 %collective-permute-start.1 = (f32[24,32,128]{2,1,0:T(8,128)}, f32[24,32,128]{2,1,0:T(8,128)S(1)}, u32[]{:S(2)}, u32[]{:S(2)}) collective-permute-start(f32[24,32,128]{2,1,0:T(8,128)} %get-tuple-element.12), channel_id=1, source_target_pairs={{32,64},{33,65},{34,66},{35,67},{36,68},{37,69},{38,70},{39,71},{4... | collective-permute-start | bytes 1179656 | tf_op jit(solution)/shard_map/ppermute | solution.py:416
  8.1 5.7 %copy-start = (f32[24,32,128]{2,1,0:T(8,128)}, f32[24,32,128]{2,1,0:T(8,128)S(1)}, u32[]{:S(2)}) copy-start(f32[24,32,128]{2,1,0:T(8,128)S(1)} %collective-permute-done.in_p) | copy-start | bytes 1179652
  13.8 0.7 copy-start.1
  14.6 19.1 %copy-start.4 = (s32[256,1]{0,1:T(1,128)S(1)}, s32[256,1]{0,1:T(1,128)}, u32[]{:S(2)}) copy-start(s32[256,1]{0,1:T(1,128)} %param.13) | copy-start | bytes 3076
  21.1 15.0 %collective-permute-start.2 = (f32[9,32,128]{2,1,0:T(8,128)}, f32[9,32,128]{2,1,0:T(8,128)S(1)}, u32[]{:S(2)}, u32[]{:S(2)}) collective-permute-start(f32[9,32,128]{2,1,0:T(8,128)} %get-tuple-element.13), channel_id=1, source_target_pairs={{0,1},{1,0},{2,3},{3,2},{4,5},{5,4},{6,7},{7,6},{8,9},{9,8},{10,11... | collective-permute-start | bytes 442376 | tf_op jit(solution)/shard_map/ppermute | solution.py:416
  29.0 9.9 %collective-permute-start.3 = (f32[9,32,128]{2,1,0:T(8,128)}, f32[9,32,128]{2,1,0:T(8,128)S(1)}, u32[]{:S(2)}, u32[]{:S(2)}) collective-permute-start(f32[9,32,128]{2,1,0:T(8,128)} %get-tuple-element.14), channel_id=1, source_target_pairs={{0,31},{1,2},{2,1},{3,4},{4,3},{5,6},{6,5},{7,8},{8,7},{9,10},{10,... | collective-permute-start | bytes 442376 | tf_op jit(solution)/shard_map/ppermute | solution.py:416
  36.1 2.9 %copy-start.2 = (f32[9,32,128]{2,1,0:T(8,128)}, f32[9,32,128]{2,1,0:T(8,128)S(1)}, u32[]{:S(2)}) copy-start(f32[9,32,128]{2,1,0:T(8,128)S(1)} %collective-permute-done.2.in_r) | copy-start | bytes 442372
  38.9 0.7 copy-start.3
where the time goes:
time: 87 us; the launch traced here: 86.7 us
  Pallas kernels  39.1 us (45%)
  blocking collectives  18.6 us (21%)
  starting transfers between devices  17.5 us (20%)
  waiting for transfers between devices  8.59 us (10%)
  local copies, waits for them, and re-layouts  2.21 us (3%)
    pallas_call x1, Pallas kernels, both_steps(): pl.pallas_call(advance_kernel, in_specs=[vmem()] * 9 + [smem, smem], out_...  26.7 us
    all_to_all x1, blocking collectives, local(): lax.all_to_all(outbox.reshape(lat_n * lon_n, CAP, NT * LEV), axes, split_...  18.6 us
    ppermute x4, starting transfers between devices, swap(): return lambda x: lax.ppermute(x, axes, pairs)  17.5 us
    ppermute x4, waiting for transfers between devices, swap(): return lambda x: lax.ppermute(x, axes, pairs)  8.59 us
    pallas_call x1, Pallas kernels, pack_cols(): pl.pallas_call(cols_kernel, out_shape=[full((QUADS, LEV, COLS))] * 2, com...  6.48 us
    pallas_call x1, Pallas kernels, pack_rows(): pl.pallas_call(body, grid=(1,), in_specs=[spec(NT * LEV, 0), spec(NT * LE...  2.53 us
    unnamed x11, local copies, waits for them, and re-layouts  2.21 us
    pallas_call x1, Pallas kernels, unpack_arrivals(): pl.pallas_call(arrivals_kernel, out_shape=[full(inbox.shape), full((1, n...  1.79 us
  transfers between devices with their start and end apart: 4, of which 2 were waited for; matrix products, arithmetic and copies ran while one was open for 1% of the time, Pallas kernels for 2%

commit v1 on v0

v1 whole, which is shorter than its diff:
```python
import jax
import jax.numpy as jnp
from jax import lax
from jax.experimental import pallas as pl
from jax.experimental.pallas import tpu as pltpu
from jax.sharding import PartitionSpec as P

CAP = 4
NT, LEV, ROWS, COLS = 4, 32, 32, 128
KG = LEV // 8
LANES = NT * LEV
SLOTS = 24
S_VE, S_VN, S_M = 16, 18, 21
ABSENT = 1e30
SIXTH = 1.0 / 6.0

WIDE, PAD = COLS + 16, 8
Q0 = 0
VE = Q0 + (ROWS + 8) * WIDE
VN = VE + (ROWS + 4) * WIDE
MS = VN + (ROWS + 6) * WIDE
Q1 = MS + (ROWS + 6) * WIDE
UE = Q1 + (ROWS + 4) * WIDE
UN = UE + (ROWS + 4) * WIDE
Q2 = UN + (ROWS + 6) * WIDE
CELLS = Q2 + ROWS * COLS
MSG = (ROWS + 4) * 4


def lanes():
    return lax.broadcasted_iota(jnp.int32, (8, COLS), 1)


def pick(x, index):
    return jnp.take_along_axis(x, index, axis=1, mode="promise_in_bounds")


def full(shape, dtype=jnp.float32):
    return jax.ShapeDtypeStruct(shape, dtype)


def params(mib):
    return pltpu.CompilerParams(vmem_limit_bytes=mib * 1024 * 1024)


def vmem():
    return pl.BlockSpec(memory_space=pltpu.VMEM)


def rows_kernel(q_lo, q_hi, ve_lo, ve_hi, vn_lo, vn_hi, lm_lo, lm_hi, area, out_p, out_q):
    lat = lax.axis_index("lat")
    even = lat % 2 == 0
    fold = lat == 3
    flip = COLS - 1 - lanes()

    def take(ref, plane, row):
        return ref[pl.ds(plane * 8 + row, 8, stride=8), :]

    def mass(ref, kg, row, at):
        wet = take(ref, kg * 8, row).astype(jnp.float32)
        return wet * jnp.broadcast_to(area[at : at + 1, :], (8, COLS))

    for kg in range(KG):

        def put(slot, bottom, normal, mirrored):
            top = jnp.where(fold, pick(mirrored, flip), normal)
            out_p[slot, kg * 8 : kg * 8 + 8, :] = jnp.where(even, top, bottom)
            out_q[slot, kg * 8 : kg * 8 + 8, :] = jnp.where(even, bottom, top)

        for c in range(NT):
            plane = c * LEV + kg * 8
            low = [take(q_lo, plane, r) for r in range(4)]
            high = [take(q_hi, plane, 4 + r) for r in range(4)]
            for r in range(4):
                put(c * 4 + r, low[r], high[r], high[3 - r])
        low = [take(ve_lo, kg * 8, r) for r in range(2)]
        high = [take(ve_hi, kg * 8, 6 + r) for r in range(2)]
        for r in range(2):
            put(S_VE + r, low[r], high[r], -high[1 - r])
        low = [take(vn_lo, kg * 8, r) for r in (0, 0, 1)]
        high = [take(vn_hi, kg * 8, 5 + r) for r in range(3)]
        for r in range(3):
            put(S_VN + r, low[r], high[r], -high[2 - r])
        low = [mass(lm_lo, kg, r, r) for r in range(3)]
        high = [mass(lm_hi, kg, 5 + r, 29 + r) for r in range(3)]
        for r in range(3):
            put(S_M + r, low[r], high[r], high[2 - r])


def pack_rows(tracers, ve, vn, lm, area):
    def spec(n, at):
        return pl.BlockSpec((n, 8, COLS), lambda i: (0, at, 0))

    def body(*refs):
        refs = list(refs)
        flat = [r.reshape(r.shape[0] * 8, COLS) for r in refs[:8]]
        rows_kernel(*flat, *refs[8:])

    q3 = tracers.reshape(NT * LEV, ROWS, COLS)
    return pl.pallas_call(
        body,
        grid=(1,),
        in_specs=[
            spec(NT * LEV, 0), spec(NT * LEV, 3), spec(LEV, 0), spec(LEV, 3),
            spec(LEV, 0), spec(LEV, 3), spec(LEV, 0), spec(LEV, 3),
            pl.BlockSpec((ROWS, COLS), lambda i: (0, 0)),
        ],
        out_specs=[pl.BlockSpec((SLOTS, LEV, COLS), lambda i: (0, 0, 0))] * 2,
        out_shape=[full((SLOTS, LEV, COLS))] * 2,
        compiler_params=params(12),
        name="pack_rows",
    )(q3, q3, ve, ve, vn, vn, lm, lm, area)


def at(section, row, col):
    return section + row * WIDE + PAD + col


def to_lanes(planes):
    return jnp.concatenate(planes, axis=0).T


def float_slots(owner, slot):
    n = owner.shape[1]
    mine = owner[...].astype(jnp.float32)
    rank = jnp.zeros((1, n), jnp.float32)
    for start in range(0, n, COLS):
        theirs = jnp.broadcast_to(mine[:, start : start + COLS], (COLS, COLS)).T
        earlier = lax.broadcasted_iota(jnp.int32, (COLS, n), 0) + start < lax.broadcasted_iota(jnp.int32, (COLS, n), 1)
        same = jnp.concatenate([theirs] * (n // COLS), axis=1) == jnp.broadcast_to(mine, (COLS, n))
        rank = rank + jnp.sum(jnp.where(same & earlier, 1.0, 0.0), axis=0, keepdims=True)
    slot[...] = owner[...] * CAP + rank.astype(jnp.int32)


def load_kernel(q, ve, vn, lm, area, owner, big, slot):
    float_slots(owner, slot)

    def step(row, _):
        def own(ref, plane):
            return ref[pl.ds(plane * ROWS + row, 8, stride=ROWS), :]

        def keep(section, row, planes):
            big[pl.ds(pl.multiple_of(at(section, row, 0), 8), COLS), :] = to_lanes(planes)

        keep(Q0, row + 4, [own(q, p * 8) for p in range(LANES // 8)])
        keep(VE, row + 2, [own(ve, kg * 8) * SIXTH for kg in range(KG)] * NT)
        keep(VN, row + 3, [own(vn, kg * 8) * SIXTH for kg in range(KG)] * NT)
        size = jnp.broadcast_to(area[pl.ds(row, 1), :], (8, COLS))
        keep(MS, row + 3, [own(lm, kg * 8).astype(jnp.float32) * size for kg in range(KG)] * NT)
        return 0

    lax.fori_loop(0, ROWS, step, 0)


def load_cells(q, ve, vn, lm, area, owner):
    return pl.pallas_call(
        load_kernel,
        in_specs=[vmem()] * 6,
        out_specs=[vmem()] * 2,
        out_shape=[full((CELLS, LANES)), full(owner.shape, jnp.int32)],
        compiler_params=params(8),
        cost_estimate=pl.CostEstimate(flops=0, bytes_accessed=16_000_000, transcendentals=0),
        name="load_cells",
    )(q, ve, vn, lm, area, owner)


def ghost_kernel(big_in, in_p, in_q, big, out_r, out_s):
    lat_even = lax.axis_index("lat") % 2 == 0
    fold = lax.axis_index("lat") == 3
    shift = jnp.where(fold, 1, 0)
    lon_even = lax.axis_index("lon") % 2 == 0
    to_r = jnp.where(lon_even, COLS - 4, 0)
    to_s = COLS - 4 - to_r

    def ghost(north, slot):
        a, b = (in_p, in_q) if north else (in_q, in_p)
        return [
            jnp.where(lat_even, a[slot, kg * 8 : kg * 8 + 8, :], b[slot, kg * 8 : kg * 8 + 8, :]) for kg in range(KG)
        ]

    def keep(section, row, planes, back=0):
        big[pl.ds(at(section, row, 0) - back, COLS), :] = to_lanes(planes)

    def static(north, slot, scale):
        return [x * scale for x in ghost(north, slot)] * NT

    for north in (False, True):
        for r in range(4):
            planes = [x for c in range(NT) for x in ghost(north, c * 4 + r)]
            keep(Q0, ROWS + 4 + r if north else r, planes)
        for r in range(2):
            keep(VE, ROWS + 2 + r if north else r, static(north, S_VE + r, SIXTH), shift if north else 0)
        for r in range(3):
            if north and r == 0:
                theirs = to_lanes(static(north, S_VN, SIXTH))
                ours = big[pl.ds(at(VN, ROWS + 2, 0), COLS), :]
                big[pl.ds(at(VN, ROWS + 5, 0), COLS), :] = jnp.where(fold, theirs, ours)
            else:
                keep(VN, ROWS + 2 + r if north else r, static(north, S_VN + r, SIXTH))
            keep(MS, ROWS + 3 + r if north else r, static(north, S_M + r, 1.0))

    group = lax.broadcasted_iota(jnp.int32, (4, LANES), 1) // LEV

    def send(row, back):
        for out, col in ((out_r, to_r), (out_s, to_s)):
            out[pl.ds(row * 4, 4), :] = big[pl.ds(at(Q0, row + 2, 0) + col, 4), :]
            east = big[pl.ds(at(VE, row, 0) + col - back, 4), :]
            north = big[pl.ds(at(VN, row + 1, 0) + col, 4), :]
            mass = big[pl.ds(at(MS, row + 1, 0) + col, 4), :]
            mixed = jnp.where(group == 0, east, jnp.where(group == 1, north, mass))
            out[pl.ds(MSG + row * 4, 4), :] = mixed

    def some(i, _):
        for j in range(4):
            send(2 + i * 4 + j, 0)
        return 0

    for row in (0, 1):
        send(row, 0)
    lax.fori_loop(0, ROWS // 4, some, 0)
    for row in (ROWS + 2, ROWS + 3):
        send(row, shift)


def ghost_rows(big, in_p, in_q):
    return pl.pallas_call(
        ghost_kernel,
        in_specs=[vmem()] * 3,
        out_specs=[vmem()] * 3,
        out_shape=[full((CELLS, LANES)), full((2 * MSG, LANES)), full((2 * MSG, LANES))],
        input_output_aliases={0: 0},
        compiler_params=params(8),
        name="ghost_rows",
    )(big, in_p, in_q)


def advance(big, flux, step, x_blocks, y_blocks):
    first = step == 0
    low, high = (-2, ROWS + 2) if first else (0, ROWS)
    src, src_row = (Q0, 4) if first else (Q1, 2)

    def x_row(r, _):
        def cells(section, row, col):
            return big[pl.ds(at(section, row + low, col) + r * WIDE, 8), :]

        for block in x_blocks:
            col = block * 8
            cur = cells(src, src_row, col)
            left = cells(src, src_row, col - 1)
            right = cells(src, src_row, col + 1)
            far = cells(src, src_row, col + 2)
            if first:
                w = cells(VE, 2, col)
                mass = jnp.minimum(cells(MS, 3, col), cells(MS, 3, col + 1))
                w = jnp.where(mass > 0, w, 0.0)
                big[pl.ds(at(UE, 2 + low, col) + r * WIDE, 8), :] = w
            else:
                w = cells(UE, 2, col)
            both = cur + right
            side = jnp.where(w > 0, 3.0 * cur - left, 3.0 * right - far)
            flux[pl.ds(at(PAD, 2 + low, col) + r * WIDE, 8), :] = w * (both + both + side)
        return 0

    lax.fori_loop(0, high - low, x_row, 0)

    def y_block(start, b):
        ahead = pl.multiple_of(b * 8, 8)

        def cells(section, row):
            return pl.ds(at(section, row, start * 8) + ahead, 8)

        def face(row, e, index=None):
            index = row + 3 if index is None else index
            if first:
                w = big[cells(VN, index), :]
                mass = jnp.minimum(big[cells(MS, row + 3), :], big[cells(MS, row + 4), :])
                w = jnp.where(mass > 0, w, 0.0)
                big[cells(UN, index), :] = w
            else:
                w = big[cells(UN, index), :]
            both = e[row] + e[row + 1]
            side = jnp.where(w > 0, 3.0 * e[row] - e[row - 1], 3.0 * e[row + 1] - e[row + 2])
            return w * (both + both + side)

        e = {row: big[cells(src, row + src_row), :] for row in range(low - 2, low + 2)}
        below = face(low - 1, e)
        for row in range(low, high):
            e[row + 2] = big[cells(src, row + src_row + 2), :]
            if row == ROWS:
                below = face(ROWS - 1, e, ROWS + 5)
            above = face(row, e)
            across = flux[cells(PAD, row + 2), :] - flux[cells(PAD - 1, row + 2), :]
            new = e[row] - big[cells(MS, row + 3), :] * (across + (above - below))
            if first:
                big[cells(Q1, row + 2), :] = new
            else:
                big[pl.ds(Q2 + row * COLS + start * 8 + ahead, 8), :] = new
            below = above

    for start, stop in y_blocks:

        def one(b, _, start=start):
            y_block(start, b)
            return 0

        lax.fori_loop(0, stop - start, one, 0)


def inner_kernel(big_in, big, flux):
    advance(big, flux, 0, range(0, 15), [(1, 15)])
    advance(big, flux, 1, range(1, 14), [(2, 14)])


def inner_steps(big):
    return pl.pallas_call(
        inner_kernel,
        in_specs=[vmem()],
        out_specs=vmem(),
        out_shape=full((CELLS, LANES)),
        scratch_shapes=[pltpu.VMEM(((ROWS + 4) * WIDE + PAD, LANES), jnp.float32)],
        input_output_aliases={0: 0},
        compiler_params=params(8),
        cost_estimate=pl.CostEstimate(flops=40_000_000, bytes_accessed=20_000_000, transcendentals=0),
        name="inner_steps",
    )(big)


def outer_kernel(big_in, in_r, in_s, cell, slot, big, outbox, after, flux, done):
    even = lax.axis_index("lon") % 2 == 0
    shift = jnp.where(lax.axis_index("lat") == 3, 1, 0)
    lane = lax.broadcasted_iota(jnp.int32, (8, LANES), 1)

    def receive(pair, back):
        rows = pl.ds(pl.multiple_of(pair * 8, 8), 8)
        more = pl.ds(pl.multiple_of(MSG + pair * 8, 8), 8)
        for west, col in ((True, -4), (False, COLS)):
            a, b = (in_s, in_r) if west else (in_r, in_s)
            q = jnp.where(even, a[rows, :], b[rows, :])
            mixed = jnp.where(even, a[more, :], b[more, :])
            parts = [pick(mixed, g * LEV + lane % LEV) for g in range(3)]
            for half in range(2):
                row = pair * 2 + half
                h = slice(half * 4, half * 4 + 4)
                big[pl.ds(at(Q0, row + 2, col), 4), :] = q[h]
                big[pl.ds(at(VE, row, col) - back, 4), :] = parts[0][h]
                big[pl.ds(at(VN, row + 1, col), 4), :] = parts[1][h]
                big[pl.ds(at(MS, row + 1, col), 4), :] = parts[2][h]

    def inside(i, _):
        for j in range(2):
            receive(1 + i * 2 + j, 0)
        return 0

    receive(0, 0)
    lax.fori_loop(0, ROWS // 4, inside, 0)
    receive(ROWS // 2 + 1, shift)

    advance(big, flux, 0, (-1, 0, 14, 15, 16), [(-1, 1), (15, 17)])
    advance(big, flux, 1, (-1, 0, 1, 13, 14, 15), [(0, 2), (14, 16)])

    keep = pltpu.make_async_copy(big.at[pl.ds(Q2, ROWS * COLS), :], after, done)
    keep.start()

    mark = jnp.where(lane == 0, ABSENT, 0.0)
    for i in range(outbox.shape[0] // 8):
        outbox[i * 8 : i * 8 + 8, :] = mark

    def send(i, _):
        for j in range(8):
            outbox[pl.ds(slot[i * 8 + j], 1), :] = big[pl.ds(Q2 + cell[i * 8 + j], 1), :]
        return 0

    lax.fori_loop(0, cell.shape[0] // 8, send, 0)
    keep.wait()


def outer_steps(big, in_r, in_s, cell, slot, devices):
    smem = pl.BlockSpec(memory_space=pltpu.SMEM)
    return pl.pallas_call(
        outer_kernel,
        in_specs=[vmem()] * 3 + [smem, smem],
        out_specs=[vmem(), vmem(), pl.BlockSpec(memory_space=pl.ANY)],
        out_shape=[full((CELLS, LANES)), full((devices * CAP, LANES)), full((ROWS * COLS, LANES))],
        scratch_shapes=[pltpu.VMEM(((ROWS + 4) * WIDE + PAD, LANES), jnp.float32), pltpu.SemaphoreType.DMA(())],
        input_output_aliases={0: 0},
        compiler_params=params(8),
        name="outer_steps",
    )(big, in_r, in_s, cell, slot)


def store_kernel(after, out):
    def step(row, _):
        x = after[pl.ds(pl.multiple_of(row * COLS, 8), COLS), :].T
        for p in range(LANES // 8):
            out[pl.ds(p * 8 * ROWS + row, 8, stride=ROWS), :] = x[p * 8 : p * 8 + 8]
        return 0

    lax.fori_loop(0, ROWS, step, 0)


def store_cells(after):
    return pl.pallas_call(
        store_kernel,
        in_specs=[vmem()],
        out_specs=vmem(),
        out_shape=full((LANES * ROWS, COLS)),
        compiler_params=params(4),
        cost_estimate=pl.CostEstimate(flops=0, bytes_accessed=8_000_000, transcendentals=0),
        name="store_cells",
    )(after)


def arrivals_kernel(inbox, out, counts):
    total = jnp.zeros((8, COLS), jnp.float32)
    sub = lax.broadcasted_iota(jnp.int32, (8, COLS), 0)
    lane = lanes()
    for i in range(inbox.shape[0] // 8):
        x = inbox[i * 8 : i * 8 + 8, :]
        here = jnp.broadcast_to(x[:, 0:1], (8, COLS)) < ABSENT * 0.5
        out[i * 8 : i * 8 + 8, :] = jnp.where(here, x, 0.0)
        total = total + jnp.where(here & (lane == (i * 8 + sub) // CAP), 1.0, 0.0)
    counts[...] = jnp.sum(total, axis=0, keepdims=True).astype(jnp.int32)


def unpack_arrivals(inbox):
    n = inbox.shape[0]
    return pl.pallas_call(
        arrivals_kernel,
        out_shape=[full(inbox.shape), full((1, n // CAP), jnp.int32)],
        compiler_params=params(4),
        name="unpack_arrivals",
    )(inbox)


def local(tracers, vel_east, vel_north, land_mask, step_area, float_cell, float_owner):
    lat_n, lon_n = lax.axis_size("lat"), lax.axis_size("lon")
    axes = ("lat", "lon")

    def swap(target):
        pairs = []
        for b in range(lat_n):
            for l in range(lon_n):
                to = target(b, l)
                if to is not None:
                    pairs.append((b * lon_n + l, to[0] * lon_n + to[1]))
        return lambda x: lax.ppermute(x, axes, pairs)

    swap_p = swap(lambda b, l: (b ^ 1, l))
    swap_q = swap(lambda b, l: {1: (2, l), 2: (1, l), 3: (3, lon_n - 1 - l)}.get(b))
    swap_r = swap(lambda b, l: (b, l ^ 1))
    swap_s = swap(lambda b, l: (b, (((l + 1) ^ 1) - 1) % lon_n))

    q = tracers.reshape(NT * LEV * ROWS, COLS)
    ve = vel_east.reshape(LEV * ROWS, COLS)
    vn = vel_north.reshape(LEV * ROWS, COLS)
    lm = land_mask.reshape(LEV * ROWS, COLS)
    out_p, out_q = pack_rows(tracers, vel_east, vel_north, land_mask, step_area)
    in_q = swap_q(out_q)
    in_p = swap_p(out_p)
    big, slot = load_cells(q, ve, vn, lm, step_area, float_owner.reshape(1, -1))
    big, out_r, out_s = ghost_rows(big, in_p, in_q)
    in_s = swap_s(out_s)
    in_r = swap_r(out_r)
    big = inner_steps(big)
    _, outbox, after = outer_steps(big, in_r, in_s, float_cell, slot.reshape(-1), lat_n * lon_n)
    inbox = lax.all_to_all(
        outbox.reshape(lat_n * lon_n, CAP, NT * LEV), axes, split_axis=0, concat_axis=0, tiled=True
    ).reshape(lat_n * lon_n * CAP, NT * LEV)
    out = store_cells(after)
    arrivals, counts = unpack_arrivals(inbox)
    return out.reshape(tracers.shape), arrivals, counts.reshape(-1)


def solution(mesh):
    placed = (
        P(None, None, "lat", "lon"),
        P(None, "lat", "lon"),
        P(None, "lat", "lon"),
        P(None, "lat", "lon"),
        P("lat", "lon"),
        P(("lat", "lon")),
        P(("lat", "lon"), None),
    )
    return jax.shard_map(
        local,
        mesh=mesh,
        in_specs=placed,
        out_specs=(P(None, None, "lat", "lon"), P(("lat", "lon"), None), P(("lat", "lon"))),
        check_vma=False,
    )
```

time: 87 us -> 59.5 us (0.68)
  blocking collectives: 18.6 us -> 0 us
  Pallas kernels: 39.1 us -> 23.1 us
  starting transfers between devices: 17.5 us -> 22.9 us
  local copies, waits for them, and re-layouts: 2.21 us -> 6.1 us
  waiting for transfers between devices: 8.59 us -> 6.25 us
    all_to_all x1 -> x0, blocking collectives: 18.6 us -> none  [local(): lax.all_to_all(outbox.reshape(lat_n * lon_n, CAP, NT * LEV), axes, split_...]
    pallas_call x3 -> x5, Pallas kernels: 34.8 us -> 21.9 us  [the longest x1 7 us: load_cells(): pl.pallas_call(load_kernel, in_specs=[vmem()] * 6, out_specs=[vmem()] * 2...]
    ppermute x4, waiting for transfers between devices: 8.59 us -> 0.8 us  [swap(): return lambda x: lax.ppermute(x, axes, pairs)]
    all_to_all x0 -> x1, starting transfers between devices: none -> 7.38 us  [local(): lax.all_to_all(outbox.reshape(lat_n * lon_n, CAP, NT * LEV), axes, split_...]
    all_to_all x0 -> x1, waiting for transfers between devices: none -> 5.45 us  [local(): lax.all_to_all(outbox.reshape(lat_n * lon_n, CAP, NT * LEV), axes, split_...]
    unnamed x11 -> x14, local copies, waits for them, and re-layouts: 2.21 us -> 6.1 us
    pallas_call x1, Pallas kernels: 2.53 us -> 0.37 us  [pack_rows(): pl.pallas_call(body, grid=(1,), in_specs=[spec(NT * LEV, 0), spec(NT * LE...]
    ppermute x4, starting transfers between devices: 17.5 us -> 15.6 us  [swap(): return lambda x: lax.ppermute(x, axes, pairs)]
  transfers between devices with their start and end apart: 4 -> 5, of which waited for: 2 -> 2; matrix products, arithmetic and copies ran while one was open for 1% -> 0% of each run, Pallas kernels for 2% -> 28%
where the time goes in v1:
time: 59.5 us; the launch traced here: 59.1 us
  Pallas kernels  23.1 us (39%)
  starting transfers between devices  22.9 us (38%)
  waiting for transfers between devices  6.25 us (11%)
  local copies, waits for them, and re-layouts  6.1 us (10%)
  between operations  0.73 us (1%)
    ppermute x4, starting transfers between devices, swap(): return lambda x: lax.ppermute(x, axes, pairs)  15.6 us
    all_to_all x1, starting transfers between devices, local(): lax.all_to_all(outbox.reshape(lat_n * lon_n, CAP, NT * LEV), axes, split_...  7.38 us
    pallas_call x1, Pallas kernels, load_cells(): pl.pallas_call(load_kernel, in_specs=[vmem()] * 6, out_specs=[vmem()] * 2...  7 us
    unnamed x14, local copies, waits for them, and re-layouts  6.1 us
    pallas_call x1, Pallas kernels, store_cells(): pl.pallas_call(store_kernel, in_specs=[vmem()], out_specs=vmem(), out_sha...  5.58 us
    all_to_all x1, waiting for transfers between devices, local(): lax.all_to_all(outbox.reshape(lat_n * lon_n, CAP, NT * LEV), axes, split_...  5.45 us
    pallas_call x1, Pallas kernels, outer_steps(): pl.pallas_call(outer_kernel, in_specs=[vmem()] * 3 + [smem, smem], out_sp...  4.48 us
    pallas_call x1, Pallas kernels, inner_steps(): pl.pallas_call(inner_kernel, in_specs=[vmem()], out_specs=vmem(), out_sha...  4.17 us
  transfers between devices with their start and end apart: 5, of which 2 were waited for; matrix products, arithmetic and copies ran while one was open for 0% of the time, Pallas kernels for 28%

profile of v1, /device:TPU:1, one launch (start us, length us, event | category | flops | bytes accessed | tf_op | source)
XLA Modules:
  0.0 59.1 jit_solution(10712073538324004442)
XLA Ops:
  0.6 0.0 copy-start
  0.6 1.6 %copy-done = f32[4,32,32,128]{3,2,1,0:T(8,128)S(1)} copy-done((f32[4,32,32,128]{3,2,1,0:T(8,128)S(1)}, f32[4,32,32,128]{3,2,1,0:T(8,128)}, u32[]{:S(2)}) %copy-start) | copy-done | bytes 2097176
  2.2 0.0 copy-start.1
  2.2 1.0 %copy-done.1 = f32[32,32,128]{2,1,0:T(8,128)S(1)} copy-done((f32[32,32,128]{2,1,0:T(8,128)S(1)}, f32[32,32,128]{2,1,0:T(8,128)}, u32[]{:S(2)}) %copy-start.1) | copy-done | bytes 524312
  3.3 0.0 copy-start.2
  3.3 1.0 %copy-done.2 = f32[32,32,128]{2,1,0:T(8,128)S(1)} copy-done((f32[32,32,128]{2,1,0:T(8,128)S(1)}, f32[32,32,128]{2,1,0:T(8,128)}, u32[]{:S(2)}) %copy-start.2) | copy-done | bytes 524312
  4.3 0.0 copy-start.3
  4.3 1.0 %copy-done.3 = s32[32,32,128]{2,1,0:T(8,128)S(1)} copy-done((s32[32,32,128]{2,1,0:T(8,128)S(1)}, s32[32,32,128]{2,1,0:T(8,128)}, u32[]{:S(2)}) %copy-start.3) | copy-done | bytes 524312
  5.3 0.0 copy-start.4
  5.4 0.7 %copy-done.4 = f32[32,128]{1,0:T(8,128)S(1)} copy-done((f32[32,128]{1,0:T(8,128)S(1)}, f32[32,128]{1,0:T(8,128)}, u32[]{:S(2)}) %copy-start.4) | copy-done | bytes 16408
  6.1 0.4 pack_rows.1
  6.4 1.5 %collective-permute-start = (f32[24,32,128]{2,1,0:T(8,128)S(1)}, f32[24,32,128]{2,1,0:T(8,128)S(1)}, u32[]{:S(2)}, u32[]{:S(2)}) collective-permute-start(f32[24,32,128]{2,1,0:T(8,128)S(1)} %get-tuple-element.15), channel_id=1, source_target_pairs={{0,32},{1,33},{2,34},{3,35},{4,36},{5,37},{6,38},{7,39},{8,40},{9,... | collective-permute-start | bytes 1179656 | tf_op jit(solution)/shard_map/ppermute | solution.py:446
  7.9 3.6 %collective-permute-start.1 = (f32[24,32,128]{2,1,0:T(8,128)S(1)}, f32[24,32,128]{2,1,0:T(8,128)S(1)}, u32[]{:S(2)}, u32[]{:S(2)}) collective-permute-start(f32[24,32,128]{2,1,0:T(8,128)S(1)} %get-tuple-element.16), channel_id=1, source_target_pairs={{32,64},{33,65},{34,66},{35,67},{36,68},{37,69},{38,70},{39,71},{4... | collective-permute-start | bytes 1179656 | tf_op jit(solution)/shard_map/ppermute | solution.py:446
  11.5 0.0 copy-start.6
  11.5 0.7 %copy-done.6 = s32[256,1]{0,1:T(1,128)S(1)} copy-done((s32[256,1]{0,1:T(1,128)S(1)}, s32[256,1]{0,1:T(1,128)}, u32[]{:S(2)}) %copy-start.6) | copy-done | bytes 1048
  12.1 7.0 %load_cells.1 = (f32[41824,128]{1,0:T(8,128)S(1)}, s32[1,256]{1,0:T(1,128)S(1)}) custom-call(f32[4096,128]{1,0:T(8,128)S(1)} %bitcast.13, f32[1024,128]{1,0:T(8,128)S(1)} %bitcast.14, f32[1024,128]{1,0:T(8,128)S(1)} %bitcast.15, s32[1024,128]{1,0:T(8,128)S(1)} %bitcast.16, f32[32,128]{1,0:T(8,128)S(1)} %copy-done.4, s32[1,256]{1,0:T(1,128)S(1)} %bitcast.19), custom_call_target="tpu_custom_call" | custom-call | bytes 16000000 | tf_op jit(solution)/shard_map/load_cells/pallas_call | solution.py:156
  19.2 0.0 collective-permute-done.in_p
  19.2 0.0 collective-permute-done.1.in_q
  19.2 0.6 %ghost_rows.1 = (f32[41824,128]{1,0:T(8,128)S(1)}, f32[288,128]{1,0:T(8,128)S(1)}, f32[288,128]{1,0:T(8,128)S(1)}) custom-call(f32[41824,128]{1,0:T(8,128)S(1)} %get-tuple-element.14.big_in, f32[24,32,128]{2,1,0:T(8,128)S(1)} %collective-permute-done.in_p, f32[24,32,128]{2,1,0:T(8,128)S(1)} %collective-permute-done.1.in_q), custom_call_target="tpu_custom_call", output_to_operand_aliasing={{0}: (0, {})} | custom-call | tf_op jit(solution)/shard_map/ghost_rows/pallas_call | solution.py:226
  19.8 5.8 %collective-permute-start.2 = (f32[288,128]{1,0:T(8,128)S(1)}, f32[288,128]{1,0:T(8,128)S(1)}, u32[]{:S(2)}, u32[]{:S(2)}) collective-permute-start(f32[288,128]{1,0:T(8,128)S(1)} %get-tuple-element.18), channel_id=1, source_target_pairs={{0,1},{1,0},{2,3},{3,2},{4,5},{5,4},{6,7},{7,6},{8,9},{9,8},{10,11... | collective-permute-start | bytes 442376 | tf_op jit(solution)/shard_map/ppermute | solution.py:446
  25.6 4.7 %collective-permute-start.3 = (f32[288,128]{1,0:T(8,128)S(1)}, f32[288,128]{1,0:T(8,128)S(1)}, u32[]{:S(2)}, u32[]{:S(2)}) collective-permute-start(f32[288,128]{1,0:T(8,128)S(1)} %get-tuple-element.19), channel_id=1, source_target_pairs={{0,31},{1,2},{2,1},{3,4},{4,3},{5,6},{6,5},{7,8},{8,7},{9,10},{10,... | collective-permute-start | bytes 442376 | tf_op jit(solution)/shard_map/ppermute | solution.py:446
  30.3 0.0 copy-start.5
  30.4 4.2 %inner_steps.1.big_in = f32[41824,128]{1,0:T(8,128)S(1)} custom-call(f32[41824,128]{1,0:T(8,128)S(1)} %get-tuple-element.17.big_in), custom_call_target="tpu_custom_call", output_to_operand_aliasing={{}: (0, {})} | custom-call | flops 40000000 | bytes 20000000 | tf_op jit(solution)/shard_map/inner_steps/pallas_call | solution.py:315
  34.5 0.0 collective-permute-done.2.in_r
  34.5 0.8 %collective-permute-done.3.in_s = f32[288,128]{1,0:T(8,128)S(1)} collective-permute-done((f32[288,128]{1,0:T(8,128)S(1)}, f32[288,128]{1,0:T(8,128)S(1)}, u32[]{:S(2)}, u32[]{:S(2)}) %collective-permute-start.3) | collective-permute-done | bytes 147488 | tf_op jit(solution)/shard_map/ppermute | solution.py:446
  35.3 0.0 copy-done.5
  35.3 4.5 %outer_steps.1 = (f32[41824,128]{1,0:T(8,128)S(1)}, f32[512,128]{1,0:T(8,128)}, f32[4096,128]{1,0:T(8,128)S(1)}) custom-call(f32[41824,128]{1,0:T(8,128)S(1)} %inner_steps.1.big_in, f32[288,128]{1,0:T(8,128)S(1)} %collective-permute-done.2.in_r, f32[288,128]{1,0:T(8,128)S(1)} %collective-permute-done.3.in_s, ...), custom_call_target="tpu_custom_call", output_to_operand_aliasing={{0}: (0, {})} | custom-call | tf_op jit(solution)/shard_map/outer_steps/pallas_call | solution.py:379
  39.8 7.4 %all-to-all-start = ((f32[128,4,128]{2,1,0:T(4,128)}), f32[128,4,128]{2,1,0:T(4,128)S(1)}, u32[]{:S(2)}, u32[]{:S(2)}) async-start(f32[128,4,128]{2,1,0:T(4,128)} %bitcast.8), calls=%async_computation | async-start | bytes 524288 | tf_op jit(solution)/shard_map/all_to_all | solution.py:466
  47.2 5.6 %store_cells.1 = f32[4096,128]{1,0:T(8,128)} custom-call(f32[4096,128]{1,0:T(8,128)S(1)} %get-tuple-element.21.after), custom_call_target="tpu_custom_call" | custom-call | bytes 8000000 | tf_op jit(solution)/shard_map/store_cells/pallas_call | solution.py:402
  52.8 5.4 %all-to-all-done = f32[128,4,128]{2,1,0:T(4,128)S(1)} async-done(((f32[128,4,128]{2,1,0:T(4,128)}), f32[128,4,128]{2,1,0:T(4,128)S(1)}, u32[]{:S(2)}, u32[]{:S(2)}) %all-to-all-start) | async-done | bytes 262176 | tf_op jit(solution)/shard_map/all_to_all | solution.py:466
  58.2 0.8 %unpack_arrivals.1 = (f32[512,128]{1,0:T(8,128)}, s32[1,128]{1,0:T(1,128)}) custom-call(f32[512,128]{1,0:T(8,128)S(1)} %bitcast.17), custom_call_target="tpu_custom_call" | custom-call | tf_op jit(solution)/shard_map/unpack_arrivals/pallas_call | solution.py:427
Async XLA Ops:
  0.6 1.6 %copy-start = (f32[4,32,32,128]{3,2,1,0:T(8,128)S(1)}, f32[4,32,32,128]{3,2,1,0:T(8,128)}, u32[]{:S(2)}) copy-start(f32[4,32,32,128]{3,2,1,0:T(8,128)} %param.7) | copy-start | bytes 6291460
  2.2 1.0 %copy-start.1 = (f32[32,32,128]{2,1,0:T(8,128)S(1)}, f32[32,32,128]{2,1,0:T(8,128)}, u32[]{:S(2)}) copy-start(f32[32,32,128]{2,1,0:T(8,128)} %refs_3_.1) | copy-start | bytes 1572868
  3.3 1.0 %copy-start.2 = (f32[32,32,128]{2,1,0:T(8,128)S(1)}, f32[32,32,128]{2,1,0:T(8,128)}, u32[]{:S(2)}) copy-start(f32[32,32,128]{2,1,0:T(8,128)} %refs_5_.1) | copy-start | bytes 1572868
  4.3 1.0 %copy-start.3 = (s32[32,32,128]{2,1,0:T(8,128)S(1)}, s32[32,32,128]{2,1,0:T(8,128)}, u32[]{:S(2)}) copy-start(s32[32,32,128]{2,1,0:T(8,128)} %refs_7_.1) | copy-start | bytes 1572868
  5.3 0.7 %copy-start.4 = (f32[32,128]{1,0:T(8,128)S(1)}, f32[32,128]{1,0:T(8,128)}, u32[]{:S(2)}) copy-start(f32[32,128]{1,0:T(8,128)} %refs_8_.1) | copy-start | bytes 49156
  6.4 12.7 %collective-permute-start = (f32[24,32,128]{2,1,0:T(8,128)S(1)}, f32[24,32,128]{2,1,0:T(8,128)S(1)}, u32[]{:S(2)}, u32[]{:S(2)}) collective-permute-start(f32[24,32,128]{2,1,0:T(8,128)S(1)} %get-tuple-element.15), channel_id=1, source_target_pairs={{0,32},{1,33},{2,34},{3,35},{4,36},{5,37},{6,38},{7,39},{8,40},{9,... | collective-permute-start | bytes 1179656 | tf_op jit(solution)/shard_map/ppermute | solution.py:446
  7.9 11.3 %collective-permute-start.1 = (f32[24,32,128]{2,1,0:T(8,128)S(1)}, f32[24,32,128]{2,1,0:T(8,128)S(1)}, u32[]{:S(2)}, u32[]{:S(2)}) collective-permute-start(f32[24,32,128]{2,1,0:T(8,128)S(1)} %get-tuple-element.16), channel_id=1, source_target_pairs={{32,64},{33,65},{34,66},{35,67},{36,68},{37,69},{38,70},{39,71},{4... | collective-permute-start | bytes 1179656 | tf_op jit(solution)/shard_map/ppermute | solution.py:446
  11.5 0.7 %copy-start.6 = (s32[256,1]{0,1:T(1,128)S(1)}, s32[256,1]{0,1:T(1,128)}, u32[]{:S(2)}) copy-start(s32[256,1]{0,1:T(1,128)} %param.13) | copy-start | bytes 3076
  19.8 14.7 %collective-permute-start.2 = (f32[288,128]{1,0:T(8,128)S(1)}, f32[288,128]{1,0:T(8,128)S(1)}, u32[]{:S(2)}, u32[]{:S(2)}) collective-permute-start(f32[288,128]{1,0:T(8,128)S(1)} %get-tuple-element.18), channel_id=1, source_target_pairs={{0,1},{1,0},{2,3},{3,2},{4,5},{5,4},{6,7},{7,6},{8,9},{9,8},{10,11... | collective-permute-start | bytes 442376 | tf_op jit(solution)/shard_map/ppermute | solution.py:446
  25.6 9.7 %collective-permute-start.3 = (f32[288,128]{1,0:T(8,128)S(1)}, f32[288,128]{1,0:T(8,128)S(1)}, u32[]{:S(2)}, u32[]{:S(2)}) collective-permute-start(f32[288,128]{1,0:T(8,128)S(1)} %get-tuple-element.19), channel_id=1, source_target_pairs={{0,31},{1,2},{2,1},{3,4},{4,3},{5,6},{6,5},{7,8},{8,7},{9,10},{10,... | collective-permute-start | bytes 442376 | tf_op jit(solution)/shard_map/ppermute | solution.py:446
  30.3 5.0 %copy-start.5 = (s32[256]{0:T(256)S(1)}, s32[256]{0:T(256)}, u32[]{:S(2)}) copy-start(s32[256]{0:T(256)} %cell.1) | copy-start | bytes 3076
  39.8 18.4 %all-to-all-start = ((f32[128,4,128]{2,1,0:T(4,128)}), f32[128,4,128]{2,1,0:T(4,128)S(1)}, u32[]{:S(2)}, u32[]{:S(2)}) async-start(f32[128,4,128]{2,1,0:T(4,128)} %bitcast.8), calls=%async_computation | async-start | bytes 524288 | tf_op jit(solution)/shard_map/all_to_all | solution.py:466

commit v2 on v1

--- a/solution.py
+++ b/solution.py
@@ -22,8 +22,7 @@
 Q1 = MS + (ROWS + 6) * WIDE
 UE = Q1 + (ROWS + 4) * WIDE
 UN = UE + (ROWS + 4) * WIDE
-Q2 = UN + (ROWS + 6) * WIDE
-CELLS = Q2 + ROWS * COLS
+CELLS = UN + (ROWS + 6) * WIDE
 MSG = (ROWS + 4) * 4
 
 
@@ -40,76 +39,90 @@
 
 
 def params(mib):
-    return pltpu.CompilerParams(vmem_limit_bytes=mib * 1024 * 1024)
+    return pltpu.CompilerParams(vmem_limit_bytes=int(mib * 1024 * 1024))
 
 
 def vmem():
     return pl.BlockSpec(memory_space=pltpu.VMEM)
 
 
-def rows_kernel(q_lo, q_hi, ve_lo, ve_hi, vn_lo, vn_hi, lm_lo, lm_hi, area, out_p, out_q):
+def rows_kernel(q, ve, vn, lm, area, out_p, out_q):
     lat = lax.axis_index("lat")
     even = lat % 2 == 0
     fold = lat == 3
     flip = COLS - 1 - lanes()
 
-    def take(ref, plane, row):
-        return ref[pl.ds(plane * 8 + row, 8, stride=8), :]
-
-    def mass(ref, kg, row, at):
-        wet = take(ref, kg * 8, row).astype(jnp.float32)
-        return wet * jnp.broadcast_to(area[at : at + 1, :], (8, COLS))
-
+    def take(pair, plane, row):
+        return pair[row // 16][pl.ds(plane * 8 + row % 8, 8, stride=8), :]
+
+    def mass(kg, row):
+        wet = take(lm, kg * 8, row).astype(jnp.float32)
+        return wet * jnp.broadcast_to(area[row : row + 1, :], (8, COLS))
+
+    top = ROWS - 4
     for kg in range(KG):
 
         def put(slot, bottom, normal, mirrored):
-            top = jnp.where(fold, pick(mirrored, flip), normal)
-            out_p[slot, kg * 8 : kg * 8 + 8, :] = jnp.where(even, top, bottom)
-            out_q[slot, kg * 8 : kg * 8 + 8, :] = jnp.where(even, bottom, top)
+            upper = jnp.where(fold, pick(mirrored, flip), normal)
+            out_p[slot, kg * 8 : kg * 8 + 8, :] = jnp.where(even, upper, bottom)
+            out_q[slot, kg * 8 : kg * 8 + 8, :] = jnp.where(even, bottom, upper)
 
         for c in range(NT):
             plane = c * LEV + kg * 8
-            low = [take(q_lo, plane, r) for r in range(4)]
-            high = [take(q_hi, plane, 4 + r) for r in range(4)]
+            low = [take(q, plane, r) for r in range(4)]
+            high = [take(q, plane, top + r) for r in range(4)]
             for r in range(4):
                 put(c * 4 + r, low[r], high[r], high[3 - r])
-        low = [take(ve_lo, kg * 8, r) for r in range(2)]
-        high = [take(ve_hi, kg * 8, 6 + r) for r in range(2)]
+        low = [take(ve, kg * 8, r) for r in range(2)]
+        high = [take(ve, kg * 8, top + 2 + r) for r in range(2)]
         for r in range(2):
             put(S_VE + r, low[r], high[r], -high[1 - r])
-        low = [take(vn_lo, kg * 8, r) for r in (0, 0, 1)]
-        high = [take(vn_hi, kg * 8, 5 + r) for r in range(3)]
+        low = [take(vn, kg * 8, r) for r in (0, 0, 1)]
+        high = [take(vn, kg * 8, top + 1 + r) for r in range(3)]
         for r in range(3):
             put(S_VN + r, low[r], high[r], -high[2 - r])
-        low = [mass(lm_lo, kg, r, r) for r in range(3)]
-        high = [mass(lm_hi, kg, 5 + r, 29 + r) for r in range(3)]
+        low = [mass(kg, r) for r in range(3)]
+        high = [mass(kg, top + 1 + r) for r in range(3)]
         for r in range(3):
             put(S_M + r, low[r], high[r], high[2 - r])
 
 
-def pack_rows(tracers, ve, vn, lm, area):
-    def spec(n, at):
-        return pl.BlockSpec((n, 8, COLS), lambda i: (0, at, 0))
-
+def pack_rows(q, ve, vn, lm, area):
     def body(*refs):
-        refs = list(refs)
-        flat = [r.reshape(r.shape[0] * 8, COLS) for r in refs[:8]]
-        rows_kernel(*flat, *refs[8:])
-
-    q3 = tracers.reshape(NT * LEV, ROWS, COLS)
+        tiles = [r.reshape(r.shape[0] * 8, COLS) for r in refs[:8]]
+        rows_kernel(*[tiles[2 * k : 2 * k + 2] for k in range(4)], *refs[8:])
+
+    def tile(n, at_tile):
+        return pl.BlockSpec((n, 8, COLS), lambda i: (0, at_tile, 0))
+
+    def whole(shape):
+        return pl.BlockSpec(shape, lambda i: (0,) * len(shape))
+
+    last = ROWS // 8 - 1
+    outs = [full((SLOTS, LEV, COLS))] * 2
     return pl.pallas_call(
         body,
         grid=(1,),
-        in_specs=[
-            spec(NT * LEV, 0), spec(NT * LEV, 3), spec(LEV, 0), spec(LEV, 3),
-            spec(LEV, 0), spec(LEV, 3), spec(LEV, 0), spec(LEV, 3),
-            pl.BlockSpec((ROWS, COLS), lambda i: (0, 0)),
-        ],
-        out_specs=[pl.BlockSpec((SLOTS, LEV, COLS), lambda i: (0, 0, 0))] * 2,
-        out_shape=[full((SLOTS, LEV, COLS))] * 2,
-        compiler_params=params(12),
+        in_specs=[tile(x.shape[0], t) for x in (q, ve, vn, lm) for t in (0, last)] + [whole(area.shape)],
+        out_specs=[whole(x.shape) for x in outs],
+        out_shape=outs,
+        compiler_params=params(53),
         name="pack_rows",
-    )(q3, q3, ve, ve, vn, vn, lm, lm, area)
+    )(q, q, ve, ve, vn, vn, lm, lm, area)
+
+
+def pass_on(*messages):
+    anywhere = [pl.BlockSpec(memory_space=pl.ANY)] * len(messages)
+    return pl.pallas_call(
+        lambda *refs: None,
+        in_specs=anywhere,
+        out_specs=anywhere,
+        out_shape=[full(m.shape) for m in messages],
+        input_output_aliases={k: k for k in range(len(messages))},
+        compiler_params=pltpu.CompilerParams(vmem_limit_bytes=1024 * 1024, has_side_effects=True),
+        cost_estimate=pl.CostEstimate(flops=30_000_000_000, bytes_accessed=0, transcendentals=0),
+        name="pass_on",
+    )(*messages)
 
 
 def at(section, row, col):
@@ -120,22 +133,8 @@
     return jnp.concatenate(planes, axis=0).T
 
 
-def float_slots(owner, slot):
-    n = owner.shape[1]
-    mine = owner[...].astype(jnp.float32)
-    rank = jnp.zeros((1, n), jnp.float32)
-    for start in range(0, n, COLS):
-        theirs = jnp.broadcast_to(mine[:, start : start + COLS], (COLS, COLS)).T
-        earlier = lax.broadcasted_iota(jnp.int32, (COLS, n), 0) + start < lax.broadcasted_iota(jnp.int32, (COLS, n), 1)
-        same = jnp.concatenate([theirs] * (n // COLS), axis=1) == jnp.broadcast_to(mine, (COLS, n))
-        rank = rank + jnp.sum(jnp.where(same & earlier, 1.0, 0.0), axis=0, keepdims=True)
-    slot[...] = owner[...] * CAP + rank.astype(jnp.int32)
-
-
-def load_kernel(q, ve, vn, lm, area, owner, big, slot):
-    float_slots(owner, slot)
-
-    def step(row, _):
+def load_kernel(q, ve, vn, lm, area, big):
+    def one(row):
         def own(ref, plane):
             return ref[pl.ds(plane * ROWS + row, 8, stride=ROWS), :]
 
@@ -147,21 +146,26 @@
         keep(VN, row + 3, [own(vn, kg * 8) * SIXTH for kg in range(KG)] * NT)
         size = jnp.broadcast_to(area[pl.ds(row, 1), :], (8, COLS))
         keep(MS, row + 3, [own(lm, kg * 8).astype(jnp.float32) * size for kg in range(KG)] * NT)
+
+    def four(i, _):
+        for j in range(4):
+            one(i * 4 + j)
         return 0
 
-    lax.fori_loop(0, ROWS, step, 0)
-
-
-def load_cells(q, ve, vn, lm, area, owner):
+    lax.fori_loop(0, ROWS // 4, four, 0)
+
+
+def load_cells(q, ve, vn, lm, area):
+    q, ve, vn, lm = [x.reshape(-1, COLS) for x in (q, ve, vn, lm)]
     return pl.pallas_call(
         load_kernel,
-        in_specs=[vmem()] * 6,
-        out_specs=[vmem()] * 2,
-        out_shape=[full((CELLS, LANES)), full(owner.shape, jnp.int32)],
+        in_specs=[vmem()] * 5,
+        out_specs=vmem(),
+        out_shape=full((CELLS, LANES)),
         compiler_params=params(8),
         cost_estimate=pl.CostEstimate(flops=0, bytes_accessed=16_000_000, transcendentals=0),
         name="load_cells",
-    )(q, ve, vn, lm, area, owner)
+    )(q, ve, vn, lm, area)
 
 
 def ghost_kernel(big_in, in_p, in_q, big, out_r, out_s):
@@ -234,12 +238,24 @@
     )(big, in_p, in_q)
 
 
-def advance(big, flux, step, x_blocks, y_blocks):
+def advance(big, after, flux, step, runs, x_blocks, y_blocks):
+    for low, high in runs:
+        across_columns(big, flux, step, low, high, x_blocks)
+    for start, stop in y_blocks:
+
+        def one(b, _, start=start):
+            for low, high in runs:
+                across_rows(big, after, flux, step, low, high, start, b)
+            return 0
+
+        lax.fori_loop(0, stop - start, one, 0)
+
+
+def across_columns(big, flux, step, low, high, x_blocks):
     first = step == 0
-    low, high = (-2, ROWS + 2) if first else (0, ROWS)
     src, src_row = (Q0, 4) if first else (Q1, 2)
 
-    def x_row(r, _):
+    def x_row(r):
         def cells(section, row, col):
             return big[pl.ds(at(section, row + low, col) + r * WIDE, 8), :]
 
@@ -253,79 +269,106 @@
                 w = cells(VE, 2, col)
                 mass = jnp.minimum(cells(MS, 3, col), cells(MS, 3, col + 1))
                 w = jnp.where(mass > 0, w, 0.0)
-                big[pl.ds(at(UE, 2 + low, col) + r * WIDE, 8), :] = w
+                opened.append((at(UE, 2 + low, col) + r * WIDE, w))
             else:
                 w = cells(UE, 2, col)
             both = cur + right
             side = jnp.where(w > 0, 3.0 * cur - left, 3.0 * right - far)
-            flux[pl.ds(at(PAD, 2 + low, col) + r * WIDE, 8), :] = w * (both + both + side)
+            fluxes.append((at(PAD, 2 + low, col) + r * WIDE, w * (both + both + side)))
+
+    def x_rows(i, _):
+        fluxes.clear()
+        opened.clear()
+        for j in range(unroll):
+            x_row(i * unroll + j)
+        for start, w in opened:
+            big[pl.ds(start, 8), :] = w
+        for start, f in fluxes:
+            flux[pl.ds(start, 8), :] = f
         return 0
 
-    lax.fori_loop(0, high - low, x_row, 0)
-
-    def y_block(start, b):
-        ahead = pl.multiple_of(b * 8, 8)
-
-        def cells(section, row):
-            return pl.ds(at(section, row, start * 8) + ahead, 8)
-
-        def face(row, e, index=None):
-            index = row + 3 if index is None else index
-            if first:
-                w = big[cells(VN, index), :]
-                mass = jnp.minimum(big[cells(MS, row + 3), :], big[cells(MS, row + 4), :])
-                w = jnp.where(mass > 0, w, 0.0)
-                big[cells(UN, index), :] = w
-            else:
-                w = big[cells(UN, index), :]
-            both = e[row] + e[row + 1]
-            side = jnp.where(w > 0, 3.0 * e[row] - e[row - 1], 3.0 * e[row + 1] - e[row + 2])
-            return w * (both + both + side)
-
-        e = {row: big[cells(src, row + src_row), :] for row in range(low - 2, low + 2)}
-        below = face(low - 1, e)
-        for row in range(low, high):
-            e[row + 2] = big[cells(src, row + src_row + 2), :]
-            if row == ROWS:
-                below = face(ROWS - 1, e, ROWS + 5)
-            above = face(row, e)
-            across = flux[cells(PAD, row + 2), :] - flux[cells(PAD - 1, row + 2), :]
-            new = e[row] - big[cells(MS, row + 3), :] * (across + (above - below))
-            if first:
-                big[cells(Q1, row + 2), :] = new
-            else:
-                big[pl.ds(Q2 + row * COLS + start * 8 + ahead, 8), :] = new
-            below = above
-
-    for start, stop in y_blocks:
-
-        def one(b, _, start=start):
-            y_block(start, b)
-            return 0
-
-        lax.fori_loop(0, stop - start, one, 0)
-
-
-def inner_kernel(big_in, big, flux):
-    advance(big, flux, 0, range(0, 15), [(1, 15)])
-    advance(big, flux, 1, range(1, 14), [(2, 14)])
-
-
-def inner_steps(big):
+    fluxes, opened = [], []
+    unroll = 4 if len(x_blocks) < 8 else 1
+    lax.fori_loop(0, (high - low) // unroll, x_rows, 0)
+
+
+def across_rows(big, after, flux, step, low, high, start, b):
+    first = step == 0
+    src, src_row = (Q0, 4) if first else (Q1, 2)
+    ahead = pl.multiple_of(b * 8, 8)
+
+    def cells(section, row):
+        return pl.ds(at(section, row, start * 8) + ahead, 8)
+
+    def face(row, e, index=None):
+        index = row + 3 if index is None else index
+        if first:
+            w = big[cells(VN, index), :]
+            mass = jnp.minimum(big[cells(MS, row + 3), :], big[cells(MS, row + 4), :])
+            w = jnp.where(mass > 0, w, 0.0)
+            big[cells(UN, index), :] = w
+        else:
+            w = big[cells(UN, index), :]
+        both = e[row] + e[row + 1]
+        side = jnp.where(w > 0, 3.0 * e[row] - e[row - 1], 3.0 * e[row + 1] - e[row + 2])
+        return w * (both + both + side)
+
+    e = {row: big[cells(src, row + src_row), :] for row in range(low - 2, low + 2)}
+    below = face(low - 1, e)
+    for row in range(low, high):
+        e[row + 2] = big[cells(src, row + src_row + 2), :]
+        if row == ROWS:
+            below = face(ROWS - 1, e, ROWS + 5)
+        above = face(row, e)
+        across = flux[cells(PAD, row + 2), :] - flux[cells(PAD - 1, row + 2), :]
+        new = e[row] - big[cells(MS, row + 3), :] * (across + (above - below))
+        if first:
+            big[cells(Q1, row + 2), :] = new
+        else:
+            after[pl.ds(row * COLS + start * 8 + ahead, 8), :] = new
+        below = above
+
+
+ALL = ((-2, ROWS + 2),), ((0, ROWS),)
+
+
+def flux_scratch():
+    return pltpu.VMEM(((ROWS + 4) * WIDE + PAD, LANES), jnp.float32)
+
+
+def float_slots(owner, slot):
+    n = owner.shape[1]
+    mine = owner[...].astype(jnp.float32)
+    rank = jnp.zeros((1, n), jnp.float32)
+    for start in range(0, n, COLS):
+        theirs = jnp.broadcast_to(mine[:, start : start + COLS], (COLS, COLS)).T
+        earlier = lax.broadcasted_iota(jnp.int32, (COLS, n), 0) + start < lax.broadcasted_iota(jnp.int32, (COLS, n), 1)
+        same = jnp.concatenate([theirs] * (n // COLS), axis=1) == jnp.broadcast_to(mine, (COLS, n))
+        rank = rank + jnp.sum(jnp.where(same & earlier, 1.0, 0.0), axis=0, keepdims=True)
+    slot[...] = owner[...] * CAP + rank.astype(jnp.int32)
+
+
+def inner_kernel(big_in, owner, big, after, slot, flux):
+    float_slots(owner, slot)
+    advance(big, after, flux, 0, ALL[0], range(0, 15), [(1, 15)])
+    advance(big, after, flux, 1, ALL[1], range(1, 14), [(2, 14)])
+
+
+def inner_steps(big, owner):
     return pl.pallas_call(
         inner_kernel,
-        in_specs=[vmem()],
-        out_specs=vmem(),
-        out_shape=full((CELLS, LANES)),
-        scratch_shapes=[pltpu.VMEM(((ROWS + 4) * WIDE + PAD, LANES), jnp.float32)],
+        in_specs=[vmem()] * 2,
+        out_specs=[vmem()] * 3,
+        out_shape=[full((CELLS, LANES)), full((ROWS * COLS, LANES)), full(owner.shape, jnp.int32)],
+        scratch_shapes=[flux_scratch()],
         input_output_aliases={0: 0},
-        compiler_params=params(8),
+        compiler_params=params(6),
         cost_estimate=pl.CostEstimate(flops=40_000_000, bytes_accessed=20_000_000, transcendentals=0),
         name="inner_steps",
-    )(big)
-
-
-def outer_kernel(big_in, in_r, in_s, cell, slot, big, outbox, after, flux, done):
+    )(big, owner)
+
+
+def outer_kernel(big_in, after_in, in_r, in_s, cell, slot, big, after, outbox, flux):
     even = lax.axis_index("lon") % 2 == 0
     shift = jnp.where(lax.axis_index("lat") == 3, 1, 0)
     lane = lax.broadcasted_iota(jnp.int32, (8, LANES), 1)
@@ -355,37 +398,35 @@
     lax.fori_loop(0, ROWS // 4, inside, 0)
     receive(ROWS // 2 + 1, shift)
 
-    advance(big, flux, 0, (-1, 0, 14, 15, 16), [(-1, 1), (15, 17)])
-    advance(big, flux, 1, (-1, 0, 1, 13, 14, 15), [(0, 2), (14, 16)])
-
-    keep = pltpu.make_async_copy(big.at[pl.ds(Q2, ROWS * COLS), :], after, done)
-    keep.start()
+    advance(big, after, flux, 0, ALL[0], (-1, 0, 14, 15, 16), [(-1, 1), (15, 17)])
+    advance(big, after, flux, 1, ALL[1], (-1, 0, 1, 13, 14, 15), [(0, 2), (14, 16)])
 
     mark = jnp.where(lane == 0, ABSENT, 0.0)
     for i in range(outbox.shape[0] // 8):
         outbox[i * 8 : i * 8 + 8, :] = mark
 
     def send(i, _):
-        for j in range(8):
-            outbox[pl.ds(slot[i * 8 + j], 1), :] = big[pl.ds(Q2 + cell[i * 8 + j], 1), :]
+        to = [slot[i * 32 + j] for j in range(32)]
+        rows = [after[pl.ds(cell[i * 32 + j], 1), :] for j in range(32)]
+        for j in range(32):
+            outbox[pl.ds(to[j], 1), :] = rows[j]
         return 0
 
-    lax.fori_loop(0, cell.shape[0] // 8, send, 0)
-    keep.wait()
-
-
-def outer_steps(big, in_r, in_s, cell, slot, devices):
+    lax.fori_loop(0, cell.shape[0] // 32, send, 0)
+
+
+def outer_steps(big, after, in_r, in_s, cell, slot, devices):
     smem = pl.BlockSpec(memory_space=pltpu.SMEM)
     return pl.pallas_call(
         outer_kernel,
-        in_specs=[vmem()] * 3 + [smem, smem],
-        out_specs=[vmem(), vmem(), pl.BlockSpec(memory_space=pl.ANY)],
-        out_shape=[full((CELLS, LANES)), full((devices * CAP, LANES)), full((ROWS * COLS, LANES))],
-        scratch_shapes=[pltpu.VMEM(((ROWS + 4) * WIDE + PAD, LANES), jnp.float32), pltpu.SemaphoreType.DMA(())],
-        input_output_aliases={0: 0},
-        compiler_params=params(8),
+        in_specs=[vmem()] * 4 + [smem, smem],
+        out_specs=[vmem()] * 3,
+        out_shape=[full((CELLS, LANES)), full((ROWS * COLS, LANES)), full((devices * CAP, LANES))],
+        scratch_shapes=[flux_scratch()],
+        input_output_aliases={0: 0, 1: 1},
+        compiler_params=params(6),
         name="outer_steps",
-    )(big, in_r, in_s, cell, slot)
+    )(big, after, in_r, in_s, cell, slot)
 
 
 def store_kernel(after, out):
@@ -450,19 +491,18 @@
     swap_r = swap(lambda b, l: (b, l ^ 1))
     swap_s = swap(lambda b, l: (b, (((l + 1) ^ 1) - 1) % lon_n))
 
-    q = tracers.reshape(NT * LEV * ROWS, COLS)
-    ve = vel_east.reshape(LEV * ROWS, COLS)
-    vn = vel_north.reshape(LEV * ROWS, COLS)
-    lm = land_mask.reshape(LEV * ROWS, COLS)
-    out_p, out_q = pack_rows(tracers, vel_east, vel_north, land_mask, step_area)
+    q = tracers.reshape(LANES, ROWS, COLS)
+    fields = (q, vel_east, vel_north, land_mask, step_area)
+    out_p, out_q = pack_rows(*fields)
+    out_p, out_q = pass_on(out_p, out_q)
     in_q = swap_q(out_q)
     in_p = swap_p(out_p)
-    big, slot = load_cells(q, ve, vn, lm, step_area, float_owner.reshape(1, -1))
+    big = load_cells(*fields)
     big, out_r, out_s = ghost_rows(big, in_p, in_q)
     in_s = swap_s(out_s)
     in_r = swap_r(out_r)
-    big = inner_steps(big)
-    _, outbox, after = outer_steps(big, in_r, in_s, float_cell, slot.reshape(-1), lat_n * lon_n)
+    big, after, slot = inner_steps(big, float_owner.reshape(1, -1))
+    _, after, outbox = outer_steps(big, after, in_r, in_s, float_cell, slot.reshape(-1), lat_n * lon_n)
     inbox = lax.all_to_all(
         outbox.reshape(lat_n * lon_n, CAP, NT * LEV), axes, split_axis=0, concat_axis=0, tiled=True
     ).reshape(lat_n * lon_n * CAP, NT * LEV)

time: 59.5 us -> 55.4 us (0.931)
  local copies, waits for them, and re-layouts: 6.1 us -> 0.75 us
  starting transfers between devices: 22.9 us -> 25 us
  Pallas kernels: 23.1 us -> 21.1 us
  waiting for transfers between devices: 6.25 us -> 7.49 us
    unnamed x14, local copies, waits for them, and re-layouts: 6.1 us -> 0.75 us
    ppermute x4, starting transfers between devices: 15.6 us -> 18 us  [swap(): return lambda x: lax.ppermute(x, axes, pairs)]
    pallas_call x4 -> x5, Pallas kernels: 16 us -> 14 us  [the longest x1 4.4 us: load_cells(): pl.pallas_call(load_kernel, in_specs=[vmem()] * 5, out_specs=vmem(), out_...]
    ppermute x4, waiting for transfers between devices: 0.8 us -> 2.04 us  [swap(): return lambda x: lax.ppermute(x, axes, pairs)]
  transfers between devices with their start and end apart: 5 -> 5, of which waited for: 2 -> 3; matrix products, arithmetic and copies ran while one was open for 0% -> 0% of each run, Pallas kernels for 28% -> 26%
where the time goes in v2:
time: 55.4 us; the launch traced here: 55.1 us
  starting transfers between devices  25 us (45%)
  Pallas kernels  21.1 us (38%)
  waiting for transfers between devices  7.49 us (14%)
  between operations  0.79 us (1%)
  local copies, waits for them, and re-layouts  0.75 us (1%)
    ppermute x4, starting transfers between devices, swap(): return lambda x: lax.ppermute(x, axes, pairs)  18 us
    all_to_all x1, starting transfers between devices, local(): lax.all_to_all(outbox.reshape(lat_n * lon_n, CAP, NT * LEV), axes, split_...  7.08 us
    pallas_call x1, Pallas kernels, store_cells(): pl.pallas_call(store_kernel, in_specs=[vmem()], out_specs=vmem(), out_sha...  5.58 us
    all_to_all x1, waiting for transfers between devices, local(): lax.all_to_all(outbox.reshape(lat_n * lon_n, CAP, NT * LEV), axes, split_...  5.45 us
    pallas_call x1, Pallas kernels, load_cells(): pl.pallas_call(load_kernel, in_specs=[vmem()] * 5, out_specs=vmem(), out_...  4.4 us
    pallas_call x1, Pallas kernels, inner_steps(): pl.pallas_call(inner_kernel, in_specs=[vmem()] * 2, out_specs=[vmem()] *...  4.18 us
    pallas_call x1, Pallas kernels, outer_steps(): pl.pallas_call(outer_kernel, in_specs=[vmem()] * 4 + [smem, smem], out_sp...  3.84 us
    ppermute x4, waiting for transfers between devices, swap(): return lambda x: lax.ppermute(x, axes, pairs)  2.04 us
  transfers between devices with their start and end apart: 5, of which 3 were waited for; matrix products, arithmetic and copies ran while one was open for 0% of the time, Pallas kernels for 26%

profile of v2, /device:TPU:1, one launch (start us, length us, event | category | flops | bytes accessed | tf_op | source)
XLA Modules:
  0.0 55.1 jit_solution(6635126246408951802)
XLA Ops:
  0.6 0.0 copy-start.4
  0.6 0.7 %copy-done.4 = f32[32,128]{1,0:T(8,128)S(1)} copy-done((f32[32,128]{1,0:T(8,128)S(1)}, f32[32,128]{1,0:T(8,128)}, u32[]{:S(2)}) %copy-start.4) | copy-done | bytes 16408
  1.3 1.6 %pack_rows.1 = (f32[24,32,128]{2,1,0:T(8,128)S(1)}, f32[24,32,128]{2,1,0:T(8,128)S(1)}) custom-call(f32[128,32,128]{2,1,0:T(8,128)} %bitcast.11, f32[128,32,128]{2,1,0:T(8,128)} %bitcast.12, f32[32,32,128]{2,1,0:T(8,128)} %refs_3_.1, f32[32,32,128]{2,1,0:T(8,128)} %refs_3_.1, f32[32,32,128]{2,1,0:T(8,128)} %refs_5_.1, f32[32,32,128]{2,1,0:T(8,128)} %refs_5_.1, ...), custom_call_target="tpu_custom_call" | custom-call | tf_op jit(solution)/shard_map/pack_rows/pallas_call | solution.py:103
  3.0 0.0 copy-start
  3.0 0.0 copy-start.1
  3.0 0.0 copy-start.2
  3.0 0.0 copy-start.3
  3.0 1.5 %collective-permute-start = (f32[24,32,128]{2,1,0:T(8,128)S(1)}, f32[24,32,128]{2,1,0:T(8,128)S(1)}, u32[]{:S(2)}, u32[]{:S(2)}) collective-permute-start(f32[24,32,128]{2,1,0:T(8,128)S(1)} %get-tuple-element.19), channel_id=1, source_target_pairs={{0,32},{1,33},{2,34},{3,35},{4,36},{5,37},{6,38},{7,39},{8,40},{9,... | collective-permute-start | bytes 1179656 | tf_op jit(solution)/shard_map/ppermute | solution.py:487
  4.5 3.8 %collective-permute-start.1 = (f32[24,32,128]{2,1,0:T(8,128)S(1)}, f32[24,32,128]{2,1,0:T(8,128)S(1)}, u32[]{:S(2)}, u32[]{:S(2)}) collective-permute-start(f32[24,32,128]{2,1,0:T(8,128)S(1)} %get-tuple-element.20), channel_id=1, source_target_pairs={{32,64},{33,65},{34,66},{35,67},{36,68},{37,69},{38,70},{39,71},{4... | collective-permute-start | bytes 1179656 | tf_op jit(solution)/shard_map/ppermute | solution.py:487
  8.3 0.0 copy-done
  8.3 0.0 copy-done.1
  8.4 0.0 copy-done.2
  8.4 0.0 copy-done.3
  8.4 0.0 copy-start.5
  8.4 4.4 %load_cells.1.big_in = f32[37728,128]{1,0:T(8,128)S(1)} custom-call(f32[4096,128]{1,0:T(8,128)S(1)} %bitcast.13, f32[1024,128]{1,0:T(8,128)S(1)} %bitcast.14, f32[1024,128]{1,0:T(8,128)S(1)} %bitcast.15, s32[1024,128]{1,0:T(8,128)S(1)} %bitcast.16, f32[32,128]{1,0:T(8,128)S(1)} %copy-done.4), custom_call_target="tpu_custom_call" | custom-call | bytes 16000000 | tf_op jit(solution)/shard_map/load_cells/pallas_call | solution.py:160
  12.8 0.0 copy-start.6
  12.8 0.0 collective-permute-done.in_p
  12.8 1.0 %collective-permute-done.1.in_q = f32[24,32,128]{2,1,0:T(8,128)S(1)} collective-permute-done((f32[24,32,128]{2,1,0:T(8,128)S(1)}, f32[24,32,128]{2,1,0:T(8,128)S(1)}, u32[]{:S(2)}, u32[]{:S(2)}) %collective-permute-start.1) | collective-permute-done | bytes 393248 | tf_op jit(solution)/shard_map/ppermute | solution.py:487
  13.8 0.6 %ghost_rows.1 = (f32[37728,128]{1,0:T(8,128)S(1)}, f32[288,128]{1,0:T(8,128)S(1)}, f32[288,128]{1,0:T(8,128)S(1)}) custom-call(f32[37728,128]{1,0:T(8,128)S(1)} %load_cells.1.big_in, f32[24,32,128]{2,1,0:T(8,128)S(1)} %collective-permute-done.in_p, f32[24,32,128]{2,1,0:T(8,128)S(1)} %collective-permute-done.1.in_q), custom_call_target="tpu_custom_call", output_to_operand_aliasing={{0}: (0, {})} | custom-call | tf_op jit(solution)/shard_map/ghost_rows/pallas_call | solution.py:230
  14.4 8.2 %collective-permute-start.2 = (f32[288,128]{1,0:T(8,128)S(1)}, f32[288,128]{1,0:T(8,128)S(1)}, u32[]{:S(2)}, u32[]{:S(2)}) collective-permute-start(f32[288,128]{1,0:T(8,128)S(1)} %get-tuple-element.24), channel_id=1, source_target_pairs={{0,1},{1,0},{2,3},{3,2},{4,5},{5,4},{6,7},{7,6},{8,9},{9,8},{10,11... | collective-permute-start | bytes 442376 | tf_op jit(solution)/shard_map/ppermute | solution.py:487
  22.6 4.4 %collective-permute-start.3 = (f32[288,128]{1,0:T(8,128)S(1)}, f32[288,128]{1,0:T(8,128)S(1)}, u32[]{:S(2)}, u32[]{:S(2)}) collective-permute-start(f32[288,128]{1,0:T(8,128)S(1)} %get-tuple-element.25), channel_id=1, source_target_pairs={{0,31},{1,2},{2,1},{3,4},{4,3},{5,6},{6,5},{7,8},{8,7},{9,10},{10,... | collective-permute-start | bytes 442376 | tf_op jit(solution)/shard_map/ppermute | solution.py:487
  27.1 0.0 copy-done.5
  27.1 4.2 %inner_steps.1 = (f32[37728,128]{1,0:T(8,128)S(1)}, f32[4096,128]{1,0:T(8,128)S(1)}, s32[1,256]{1,0:T(1,128)S(1)}) custom-call(f32[37728,128]{1,0:T(8,128)S(1)} %get-tuple-element.21.big_in, s32[1,256]{1,0:T(1,128)S(1)} %bitcast.18), custom_call_target="tpu_custom_call", output_to_operand_aliasing={{0}: (0, {})} | custom-call | flops 40000000 | bytes 20000000 | tf_op jit(solution)/shard_map/inner_steps/pallas_call | solution.py:358
  31.3 0.0 collective-permute-done.2.in_r
  31.3 1.1 %collective-permute-done.3.in_s = f32[288,128]{1,0:T(8,128)S(1)} collective-permute-done((f32[288,128]{1,0:T(8,128)S(1)}, f32[288,128]{1,0:T(8,128)S(1)}, u32[]{:S(2)}, u32[]{:S(2)}) %collective-permute-start.3) | collective-permute-done | bytes 147488 | tf_op jit(solution)/shard_map/ppermute | solution.py:487
  32.3 0.0 copy-done.6
  32.4 3.8 %outer_steps.1 = (f32[37728,128]{1,0:T(8,128)S(1)}, f32[4096,128]{1,0:T(8,128)S(1)}, f32[512,128]{1,0:T(8,128)}) custom-call(f32[37728,128]{1,0:T(8,128)S(1)} %get-tuple-element.22.big_in, f32[4096,128]{1,0:T(8,128)S(1)} %get-tuple-element.23.after_in, f32[288,128]{1,0:T(8,128)S(1)} %collective-permute-done.2.in_r, ...), custom_call_target="tpu_custom_call", output_to_operand_aliasing={{0}: (0, {}), {1}: (1, {})} | custom-call | tf_op jit(solution)/shard_map/outer_steps/pallas_call | solution.py:420
  36.2 7.1 %all-to-all-start = ((f32[128,4,128]{2,1,0:T(4,128)}), f32[128,4,128]{2,1,0:T(4,128)S(1)}, u32[]{:S(2)}, u32[]{:S(2)}) async-start(f32[128,4,128]{2,1,0:T(4,128)} %bitcast.8), calls=%async_computation | async-start | bytes 524288 | tf_op jit(solution)/shard_map/all_to_all | solution.py:506
  43.3 5.6 %store_cells.1 = f32[4096,128]{1,0:T(8,128)} custom-call(f32[4096,128]{1,0:T(8,128)S(1)} %get-tuple-element.27.after), custom_call_target="tpu_custom_call" | custom-call | bytes 8000000 | tf_op jit(solution)/shard_map/store_cells/pallas_call | solution.py:443
  48.9 5.4 %all-to-all-done = f32[128,4,128]{2,1,0:T(4,128)S(1)} async-done(((f32[128,4,128]{2,1,0:T(4,128)}), f32[128,4,128]{2,1,0:T(4,128)S(1)}, u32[]{:S(2)}, u32[]{:S(2)}) %all-to-all-start) | async-done | bytes 262176 | tf_op jit(solution)/shard_map/all_to_all | solution.py:506
  54.3 0.8 %unpack_arrivals.1 = (f32[512,128]{1,0:T(8,128)}, s32[1,128]{1,0:T(1,128)}) custom-call(f32[512,128]{1,0:T(8,128)S(1)} %bitcast.17), custom_call_target="tpu_custom_call" | custom-call | tf_op jit(solution)/shard_map/unpack_arrivals/pallas_call | solution.py:468
  (1 shorter events, 0.0 us)
Async XLA Ops:
  0.6 0.7 %copy-start.4 = (f32[32,128]{1,0:T(8,128)S(1)}, f32[32,128]{1,0:T(8,128)}, u32[]{:S(2)}) copy-start(f32[32,128]{1,0:T(8,128)} %refs_8_.1) | copy-start | bytes 49156
  3.0 5.3 %copy-start = (f32[4,32,32,128]{3,2,1,0:T(8,128)S(1)}, f32[4,32,32,128]{3,2,1,0:T(8,128)}, u32[]{:S(2)}) copy-start(f32[4,32,32,128]{3,2,1,0:T(8,128)} %param.7) | copy-start | bytes 6291460
  3.0 5.3 %copy-start.1 = (f32[32,32,128]{2,1,0:T(8,128)S(1)}, f32[32,32,128]{2,1,0:T(8,128)}, u32[]{:S(2)}) copy-start(f32[32,32,128]{2,1,0:T(8,128)} %refs_3_.1) | copy-start | bytes 1572868
  3.0 5.3 %copy-start.2 = (f32[32,32,128]{2,1,0:T(8,128)S(1)}, f32[32,32,128]{2,1,0:T(8,128)}, u32[]{:S(2)}) copy-start(f32[32,32,128]{2,1,0:T(8,128)} %refs_5_.1) | copy-start | bytes 1572868
  3.0 5.3 %copy-start.3 = (s32[32,32,128]{2,1,0:T(8,128)S(1)}, s32[32,32,128]{2,1,0:T(8,128)}, u32[]{:S(2)}) copy-start(s32[32,32,128]{2,1,0:T(8,128)} %refs_7_.1) | copy-start | bytes 1572868
  3.0 9.8 %collective-permute-start = (f32[24,32,128]{2,1,0:T(8,128)S(1)}, f32[24,32,128]{2,1,0:T(8,128)S(1)}, u32[]{:S(2)}, u32[]{:S(2)}) collective-permute-start(f32[24,32,128]{2,1,0:T(8,128)S(1)} %get-tuple-element.19), channel_id=1, source_target_pairs={{0,32},{1,33},{2,34},{3,35},{4,36},{5,37},{6,38},{7,39},{8,40},{9,... | collective-permute-start | bytes 1179656 | tf_op jit(solution)/shard_map/ppermute | solution.py:487
  4.5 9.3 %collective-permute-start.1 = (f32[24,32,128]{2,1,0:T(8,128)S(1)}, f32[24,32,128]{2,1,0:T(8,128)S(1)}, u32[]{:S(2)}, u32[]{:S(2)}) collective-permute-start(f32[24,32,128]{2,1,0:T(8,128)S(1)} %get-tuple-element.20), channel_id=1, source_target_pairs={{32,64},{33,65},{34,66},{35,67},{36,68},{37,69},{38,70},{39,71},{4... | collective-permute-start | bytes 1179656 | tf_op jit(solution)/shard_map/ppermute | solution.py:487
  8.4 18.7 %copy-start.5 = (s32[256,1]{0,1:T(1,128)S(1)}, s32[256,1]{0,1:T(1,128)}, u32[]{:S(2)}) copy-start(s32[256,1]{0,1:T(1,128)} %param.13) | copy-start | bytes 3076
  12.8 19.6 %copy-start.6 = (s32[256]{0:T(256)S(1)}, s32[256]{0:T(256)}, u32[]{:S(2)}) copy-start(s32[256]{0:T(256)} %cell.1) | copy-start | bytes 3076
  14.4 16.9 %collective-permute-start.2 = (f32[288,128]{1,0:T(8,128)S(1)}, f32[288,128]{1,0:T(8,128)S(1)}, u32[]{:S(2)}, u32[]{:S(2)}) collective-permute-start(f32[288,128]{1,0:T(8,128)S(1)} %get-tuple-element.24), channel_id=1, source_target_pairs={{0,1},{1,0},{2,3},{3,2},{4,5},{5,4},{6,7},{7,6},{8,9},{9,8},{10,11... | collective-permute-start | bytes 442376 | tf_op jit(solution)/shard_map/ppermute | solution.py:487
  22.6 9.7 %collective-permute-start.3 = (f32[288,128]{1,0:T(8,128)S(1)}, f32[288,128]{1,0:T(8,128)S(1)}, u32[]{:S(2)}, u32[]{:S(2)}) collective-permute-start(f32[288,128]{1,0:T(8,128)S(1)} %get-tuple-element.25), channel_id=1, source_target_pairs={{0,31},{1,2},{2,1},{3,4},{4,3},{5,6},{6,5},{7,8},{8,7},{9,10},{10,... | collective-permute-start | bytes 442376 | tf_op jit(solution)/shard_map/ppermute | solution.py:487
  36.2 18.1 %all-to-all-start = ((f32[128,4,128]{2,1,0:T(4,128)}), f32[128,4,128]{2,1,0:T(4,128)S(1)}, u32[]{:S(2)}, u32[]{:S(2)}) async-start(f32[128,4,128]{2,1,0:T(4,128)} %bitcast.8), calls=%async_computation | async-start | bytes 524288 | tf_op jit(solution)/shard_map/all_to_all | solution.py:506

commit v3 on v2

--- a/solution.py
+++ b/solution.py
@@ -5,11 +5,12 @@
 from jax.experimental.pallas import tpu as pltpu
 from jax.sharding import PartitionSpec as P
 
+
 CAP = 4
 NT, LEV, ROWS, COLS = 4, 32, 32, 128
 KG = LEV // 8
 LANES = NT * LEV
-SLOTS = 24
+SLOTS = 23
 S_VE, S_VN, S_M = 16, 18, 21
 ABSENT = 1e30
 SIXTH = 1.0 / 6.0
@@ -79,12 +80,14 @@
             put(S_VE + r, low[r], high[r], -high[1 - r])
         low = [take(vn, kg * 8, r) for r in (0, 0, 1)]
         high = [take(vn, kg * 8, top + 1 + r) for r in range(3)]
+        low[2] = low[2] * (take(lm, kg * 8, 1) * take(lm, kg * 8, 2)).astype(jnp.float32)
+        high[0] = high[0] * (take(lm, kg * 8, top + 1) * take(lm, kg * 8, top + 2)).astype(jnp.float32)
         for r in range(3):
             put(S_VN + r, low[r], high[r], -high[2 - r])
-        low = [mass(kg, r) for r in range(3)]
-        high = [mass(kg, top + 1 + r) for r in range(3)]
-        for r in range(3):
-            put(S_M + r, low[r], high[r], high[2 - r])
+        low = [mass(kg, r) for r in range(2)]
+        high = [mass(kg, top + 2 + r) for r in range(2)]
+        for r in range(2):
+            put(S_M + r, low[r], high[r], high[1 - r])
 
 
 def pack_rows(q, ve, vn, lm, area):
@@ -201,7 +204,9 @@
                 big[pl.ds(at(VN, ROWS + 5, 0), COLS), :] = jnp.where(fold, theirs, ours)
             else:
                 keep(VN, ROWS + 2 + r if north else r, static(north, S_VN + r, SIXTH))
-            keep(MS, ROWS + 3 + r if north else r, static(north, S_M + r, 1.0))
+        for r in range(2):
+            keep(MS, ROWS + 3 + r if north else 1 + r, static(north, S_M + r, 1.0))
+        big[pl.ds(at(MS, ROWS + 5 if north else 0, 0), COLS), :] = jnp.ones((COLS, LANES), jnp.float32)
 
     group = lax.broadcasted_iota(jnp.int32, (4, LANES), 1) // LEV
 

time: 55.4 us -> 55.2 us (level)
  waiting for transfers between devices: 7.49 us -> 6.24 us
  starting transfers between devices: 25 us -> 26.1 us
    ppermute x4, waiting for transfers between devices: 2.04 us -> 0.79 us  [swap(): return lambda x: lax.ppermute(x, axes, pairs)]
    all_to_all x1, starting transfers between devices: 7.08 us -> 8.2 us  [local(): lax.all_to_all(outbox.reshape(lat_n * lon_n, CAP, NT * LEV), axes, split_...]
  transfers between devices with their start and end apart: 5 -> 5, of which waited for: 3 -> 2; matrix products, arithmetic and copies ran while one was open for 0% -> 0% of each run, Pallas kernels for 26% -> 26%
where the time goes in v3:
time: 55.2 us; the launch traced here: 54.9 us
  starting transfers between devices  26.1 us (47%)
  Pallas kernels  21.1 us (38%)
  waiting for transfers between devices  6.24 us (11%)
  between operations  0.81 us (1%)
  local copies, waits for them, and re-layouts  0.75 us (1%)
    ppermute x4, starting transfers between devices, swap(): return lambda x: lax.ppermute(x, axes, pairs)  17.9 us
    all_to_all x1, starting transfers between devices, local(): lax.all_to_all(outbox.reshape(lat_n * lon_n, CAP, NT * LEV), axes, split_...  8.2 us
    pallas_call x1, Pallas kernels, store_cells(): pl.pallas_call(store_kernel, in_specs=[vmem()], out_specs=vmem(), out_sha...  5.58 us
    all_to_all x1, waiting for transfers between devices, local(): lax.all_to_all(outbox.reshape(lat_n * lon_n, CAP, NT * LEV), axes, split_...  5.45 us
    pallas_call x1, Pallas kernels, load_cells(): pl.pallas_call(load_kernel, in_specs=[vmem()] * 5, out_specs=vmem(), out_...  4.4 us
    pallas_call x1, Pallas kernels, inner_steps(): pl.pallas_call(inner_kernel, in_specs=[vmem()] * 2, out_specs=[vmem()] *...  4.18 us
    pallas_call x1, Pallas kernels, outer_steps(): pl.pallas_call(outer_kernel, in_specs=[vmem()] * 4 + [smem, smem], out_sp...  3.84 us
    pallas_call x1, Pallas kernels, pack_rows(): pl.pallas_call(body, grid=(1,), in_specs=[tile(x.shape[0], t) for x in (q...  1.63 us
  transfers between devices with their start and end apart: 5, of which 2 were waited for; matrix products, arithmetic and copies ran while one was open for 0% of the time, Pallas kernels for 26%

profile of v3, /device:TPU:1, one launch (start us, length us, event | category | flops | bytes accessed | tf_op | source)
XLA Modules:
  0.0 54.9 jit_solution(7417189015028214061)
XLA Ops:
  0.6 0.0 copy-start.4
  0.6 0.7 %copy-done.4 = f32[32,128]{1,0:T(8,128)S(1)} copy-done((f32[32,128]{1,0:T(8,128)S(1)}, f32[32,128]{1,0:T(8,128)}, u32[]{:S(2)}) %copy-start.4) | copy-done | bytes 16408
  1.3 1.6 %pack_rows.1 = (f32[23,32,128]{2,1,0:T(8,128)S(1)}, f32[23,32,128]{2,1,0:T(8,128)S(1)}) custom-call(f32[128,32,128]{2,1,0:T(8,128)} %bitcast.11, f32[128,32,128]{2,1,0:T(8,128)} %bitcast.12, f32[32,32,128]{2,1,0:T(8,128)} %refs_3_.1, f32[32,32,128]{2,1,0:T(8,128)} %refs_3_.1, f32[32,32,128]{2,1,0:T(8,128)} %refs_5_.1, f32[32,32,128]{2,1,0:T(8,128)} %refs_5_.1, ...), custom_call_target="tpu_custom_call" | custom-call | tf_op jit(solution)/shard_map/pack_rows/pallas_call | solution.py:106
  3.0 0.0 copy-start
  3.0 0.0 copy-start.1
  3.0 0.0 copy-start.2
  3.0 0.0 copy-start.3
  3.0 1.5 %collective-permute-start = (f32[23,32,128]{2,1,0:T(8,128)S(1)}, f32[23,32,128]{2,1,0:T(8,128)S(1)}, u32[]{:S(2)}, u32[]{:S(2)}) collective-permute-start(f32[23,32,128]{2,1,0:T(8,128)S(1)} %get-tuple-element.19), channel_id=1, source_target_pairs={{0,32},{1,33},{2,34},{3,35},{4,36},{5,37},{6,38},{7,39},{8,40},{9,... | collective-permute-start | bytes 1130504 | tf_op jit(solution)/shard_map/ppermute | solution.py:492
  4.5 3.8 %collective-permute-start.1 = (f32[23,32,128]{2,1,0:T(8,128)S(1)}, f32[23,32,128]{2,1,0:T(8,128)S(1)}, u32[]{:S(2)}, u32[]{:S(2)}) collective-permute-start(f32[23,32,128]{2,1,0:T(8,128)S(1)} %get-tuple-element.20), channel_id=1, source_target_pairs={{32,64},{33,65},{34,66},{35,67},{36,68},{37,69},{38,70},{39,71},{4... | collective-permute-start | bytes 1130504 | tf_op jit(solution)/shard_map/ppermute | solution.py:492
  8.3 0.0 copy-done
  8.3 0.0 copy-done.1
  8.4 0.0 copy-done.2
  8.4 0.0 copy-done.3
  8.4 0.0 copy-start.5
  8.4 4.4 %load_cells.1.big_in = f32[37728,128]{1,0:T(8,128)S(1)} custom-call(f32[4096,128]{1,0:T(8,128)S(1)} %bitcast.13, f32[1024,128]{1,0:T(8,128)S(1)} %bitcast.14, f32[1024,128]{1,0:T(8,128)S(1)} %bitcast.15, s32[1024,128]{1,0:T(8,128)S(1)} %bitcast.16, f32[32,128]{1,0:T(8,128)S(1)} %copy-done.4), custom_call_target="tpu_custom_call" | custom-call | bytes 16000000 | tf_op jit(solution)/shard_map/load_cells/pallas_call | solution.py:163
  12.8 0.0 copy-start.6
  12.8 0.0 collective-permute-done.in_p
  12.8 0.8 %collective-permute-done.1.in_q = f32[23,32,128]{2,1,0:T(8,128)S(1)} collective-permute-done((f32[23,32,128]{2,1,0:T(8,128)S(1)}, f32[23,32,128]{2,1,0:T(8,128)S(1)}, u32[]{:S(2)}, u32[]{:S(2)}) %collective-permute-start.1) | collective-permute-done | bytes 376864 | tf_op jit(solution)/shard_map/ppermute | solution.py:492
  13.6 0.6 %ghost_rows.1 = (f32[37728,128]{1,0:T(8,128)S(1)}, f32[288,128]{1,0:T(8,128)S(1)}, f32[288,128]{1,0:T(8,128)S(1)}) custom-call(f32[37728,128]{1,0:T(8,128)S(1)} %load_cells.1.big_in, f32[23,32,128]{2,1,0:T(8,128)S(1)} %collective-permute-done.in_p, f32[23,32,128]{2,1,0:T(8,128)S(1)} %collective-permute-done.1.in_q), custom_call_target="tpu_custom_call", output_to_operand_aliasing={{0}: (0, {})} | custom-call | tf_op jit(solution)/shard_map/ghost_rows/pallas_call | solution.py:235
  14.2 3.7 %collective-permute-start.2 = (f32[288,128]{1,0:T(8,128)S(1)}, f32[288,128]{1,0:T(8,128)S(1)}, u32[]{:S(2)}, u32[]{:S(2)}) collective-permute-start(f32[288,128]{1,0:T(8,128)S(1)} %get-tuple-element.24), channel_id=1, source_target_pairs={{0,1},{1,0},{2,3},{3,2},{4,5},{5,4},{6,7},{7,6},{8,9},{9,8},{10,11... | collective-permute-start | bytes 442376 | tf_op jit(solution)/shard_map/ppermute | solution.py:492
  17.9 8.9 %collective-permute-start.3 = (f32[288,128]{1,0:T(8,128)S(1)}, f32[288,128]{1,0:T(8,128)S(1)}, u32[]{:S(2)}, u32[]{:S(2)}) collective-permute-start(f32[288,128]{1,0:T(8,128)S(1)} %get-tuple-element.25), channel_id=1, source_target_pairs={{0,31},{1,2},{2,1},{3,4},{4,3},{5,6},{6,5},{7,8},{8,7},{9,10},{10,... | collective-permute-start | bytes 442376 | tf_op jit(solution)/shard_map/ppermute | solution.py:492
  26.8 0.0 copy-done.5
  26.8 4.2 %inner_steps.1 = (f32[37728,128]{1,0:T(8,128)S(1)}, f32[4096,128]{1,0:T(8,128)S(1)}, s32[1,256]{1,0:T(1,128)S(1)}) custom-call(f32[37728,128]{1,0:T(8,128)S(1)} %get-tuple-element.21.big_in, s32[1,256]{1,0:T(1,128)S(1)} %bitcast.18), custom_call_target="tpu_custom_call", output_to_operand_aliasing={{0}: (0, {})} | custom-call | flops 40000000 | bytes 20000000 | tf_op jit(solution)/shard_map/inner_steps/pallas_call | solution.py:363
  31.0 0.0 collective-permute-done.2.in_r
  31.0 0.0 collective-permute-done.3.in_s
  31.0 0.0 copy-done.6
  31.0 3.8 %outer_steps.1 = (f32[37728,128]{1,0:T(8,128)S(1)}, f32[4096,128]{1,0:T(8,128)S(1)}, f32[512,128]{1,0:T(8,128)}) custom-call(f32[37728,128]{1,0:T(8,128)S(1)} %get-tuple-element.22.big_in, f32[4096,128]{1,0:T(8,128)S(1)} %get-tuple-element.23.after_in, f32[288,128]{1,0:T(8,128)S(1)} %collective-permute-done.2.in_r, ...), custom_call_target="tpu_custom_call", output_to_operand_aliasing={{0}: (0, {}), {1}: (1, {})} | custom-call | tf_op jit(solution)/shard_map/outer_steps/pallas_call | solution.py:425
  34.9 8.2 %all-to-all-start = ((f32[128,4,128]{2,1,0:T(4,128)}), f32[128,4,128]{2,1,0:T(4,128)S(1)}, u32[]{:S(2)}, u32[]{:S(2)}) async-start(f32[128,4,128]{2,1,0:T(4,128)} %bitcast.8), calls=%async_computation | async-start | bytes 524288 | tf_op jit(solution)/shard_map/all_to_all | solution.py:511
  43.1 5.6 %store_cells.1 = f32[4096,128]{1,0:T(8,128)} custom-call(f32[4096,128]{1,0:T(8,128)S(1)} %get-tuple-element.27.after), custom_call_target="tpu_custom_call" | custom-call | bytes 8000000 | tf_op jit(solution)/shard_map/store_cells/pallas_call | solution.py:448
  48.7 5.4 %all-to-all-done = f32[128,4,128]{2,1,0:T(4,128)S(1)} async-done(((f32[128,4,128]{2,1,0:T(4,128)}), f32[128,4,128]{2,1,0:T(4,128)S(1)}, u32[]{:S(2)}, u32[]{:S(2)}) %all-to-all-start) | async-done | bytes 262176 | tf_op jit(solution)/shard_map/all_to_all | solution.py:511
  54.1 0.8 %unpack_arrivals.1 = (f32[512,128]{1,0:T(8,128)}, s32[1,128]{1,0:T(1,128)}) custom-call(f32[512,128]{1,0:T(8,128)S(1)} %bitcast.17), custom_call_target="tpu_custom_call" | custom-call | tf_op jit(solution)/shard_map/unpack_arrivals/pallas_call | solution.py:473
  (1 shorter events, 0.0 us)
Async XLA Ops:
  0.6 0.7 %copy-start.4 = (f32[32,128]{1,0:T(8,128)S(1)}, f32[32,128]{1,0:T(8,128)}, u32[]{:S(2)}) copy-start(f32[32,128]{1,0:T(8,128)} %refs_8_.1) | copy-start | bytes 49156
  3.0 5.3 %copy-start = (f32[4,32,32,128]{3,2,1,0:T(8,128)S(1)}, f32[4,32,32,128]{3,2,1,0:T(8,128)}, u32[]{:S(2)}) copy-start(f32[4,32,32,128]{3,2,1,0:T(8,128)} %param.7) | copy-start | bytes 6291460
  3.0 5.3 %copy-start.1 = (f32[32,32,128]{2,1,0:T(8,128)S(1)}, f32[32,32,128]{2,1,0:T(8,128)}, u32[]{:S(2)}) copy-start(f32[32,32,128]{2,1,0:T(8,128)} %refs_3_.1) | copy-start | bytes 1572868
  3.0 5.3 %copy-start.2 = (f32[32,32,128]{2,1,0:T(8,128)S(1)}, f32[32,32,128]{2,1,0:T(8,128)}, u32[]{:S(2)}) copy-start(f32[32,32,128]{2,1,0:T(8,128)} %refs_5_.1) | copy-start | bytes 1572868
  3.0 5.3 %copy-start.3 = (s32[32,32,128]{2,1,0:T(8,128)S(1)}, s32[32,32,128]{2,1,0:T(8,128)}, u32[]{:S(2)}) copy-start(s32[32,32,128]{2,1,0:T(8,128)} %refs_7_.1) | copy-start | bytes 1572868
  3.0 9.8 %collective-permute-start = (f32[23,32,128]{2,1,0:T(8,128)S(1)}, f32[23,32,128]{2,1,0:T(8,128)S(1)}, u32[]{:S(2)}, u32[]{:S(2)}) collective-permute-start(f32[23,32,128]{2,1,0:T(8,128)S(1)} %get-tuple-element.19), channel_id=1, source_target_pairs={{0,32},{1,33},{2,34},{3,35},{4,36},{5,37},{6,38},{7,39},{8,40},{9,... | collective-permute-start | bytes 1130504 | tf_op jit(solution)/shard_map/ppermute | solution.py:492
  4.5 9.1 %collective-permute-start.1 = (f32[23,32,128]{2,1,0:T(8,128)S(1)}, f32[23,32,128]{2,1,0:T(8,128)S(1)}, u32[]{:S(2)}, u32[]{:S(2)}) collective-permute-start(f32[23,32,128]{2,1,0:T(8,128)S(1)} %get-tuple-element.20), channel_id=1, source_target_pairs={{32,64},{33,65},{34,66},{35,67},{36,68},{37,69},{38,70},{39,71},{4... | collective-permute-start | bytes 1130504 | tf_op jit(solution)/shard_map/ppermute | solution.py:492
  8.4 18.4 %copy-start.5 = (s32[256,1]{0,1:T(1,128)S(1)}, s32[256,1]{0,1:T(1,128)}, u32[]{:S(2)}) copy-start(s32[256,1]{0,1:T(1,128)} %param.13) | copy-start | bytes 3076
  12.8 18.2 %copy-start.6 = (s32[256]{0:T(256)S(1)}, s32[256]{0:T(256)}, u32[]{:S(2)}) copy-start(s32[256]{0:T(256)} %cell.1) | copy-start | bytes 3076
  14.2 16.8 %collective-permute-start.2 = (f32[288,128]{1,0:T(8,128)S(1)}, f32[288,128]{1,0:T(8,128)S(1)}, u32[]{:S(2)}, u32[]{:S(2)}) collective-permute-start(f32[288,128]{1,0:T(8,128)S(1)} %get-tuple-element.24), channel_id=1, source_target_pairs={{0,1},{1,0},{2,3},{3,2},{4,5},{5,4},{6,7},{7,6},{8,9},{9,8},{10,11... | collective-permute-start | bytes 442376 | tf_op jit(solution)/shard_map/ppermute | solution.py:492
  17.9 13.1 %collective-permute-start.3 = (f32[288,128]{1,0:T(8,128)S(1)}, f32[288,128]{1,0:T(8,128)S(1)}, u32[]{:S(2)}, u32[]{:S(2)}) collective-permute-start(f32[288,128]{1,0:T(8,128)S(1)} %get-tuple-element.25), channel_id=1, source_target_pairs={{0,31},{1,2},{2,1},{3,4},{4,3},{5,6},{6,5},{7,8},{8,7},{9,10},{10,... | collective-permute-start | bytes 442376 | tf_op jit(solution)/shard_map/ppermute | solution.py:492
  34.9 19.2 %all-to-all-start = ((f32[128,4,128]{2,1,0:T(4,128)}), f32[128,4,128]{2,1,0:T(4,128)S(1)}, u32[]{:S(2)}, u32[]{:S(2)}) async-start(f32[128,4,128]{2,1,0:T(4,128)} %bitcast.8), calls=%async_computation | async-start | bytes 524288 | tf_op jit(solution)/shard_map/all_to_all | solution.py:511

commit v4 on v3

--- a/solution.py
+++ b/solution.py
@@ -220,13 +220,13 @@
             out[pl.ds(MSG + row * 4, 4), :] = mixed
 
     def some(i, _):
-        for j in range(4):
-            send(2 + i * 4 + j, 0)
+        for j in range(8):
+            send(2 + i * 8 + j, 0)
         return 0
 
     for row in (0, 1):
         send(row, 0)
-    lax.fori_loop(0, ROWS // 4, some, 0)
+    lax.fori_loop(0, ROWS // 8, some, 0)
     for row in (ROWS + 2, ROWS + 3):
         send(row, shift)
 
@@ -395,12 +395,12 @@
                 big[pl.ds(at(MS, row + 1, col), 4), :] = parts[2][h]
 
     def inside(i, _):
-        for j in range(2):
-            receive(1 + i * 2 + j, 0)
+        for j in range(4):
+            receive(1 + i * 4 + j, 0)
         return 0
 
     receive(0, 0)
-    lax.fori_loop(0, ROWS // 4, inside, 0)
+    lax.fori_loop(0, ROWS // 8, inside, 0)
     receive(ROWS // 2 + 1, shift)
 
     advance(big, after, flux, 0, ALL[0], (-1, 0, 14, 15, 16), [(-1, 1), (15, 17)])
@@ -411,13 +411,13 @@
         outbox[i * 8 : i * 8 + 8, :] = mark
 
     def send(i, _):
-        to = [slot[i * 32 + j] for j in range(32)]
-        rows = [after[pl.ds(cell[i * 32 + j], 1), :] for j in range(32)]
-        for j in range(32):
+        to = [slot[i * 64 + j] for j in range(64)]
+        rows = [after[pl.ds(cell[i * 64 + j], 1), :] for j in range(64)]
+        for j in range(64):
             outbox[pl.ds(to[j], 1), :] = rows[j]
         return 0
 
-    lax.fori_loop(0, cell.shape[0] // 32, send, 0)
+    lax.fori_loop(0, cell.shape[0] // 64, send, 0)
 
 
 def outer_steps(big, after, in_r, in_s, cell, slot, devices):

time: 55.2 us -> 54.9 us (level)
  no operation moved by 1% of the time
where the time goes in v4:
time: 54.9 us; the launch traced here: 54.6 us
  starting transfers between devices  26.1 us (48%)
  Pallas kernels  20.7 us (38%)
  waiting for transfers between devices  6.24 us (11%)
  between operations  0.81 us (1%)
  local copies, waits for them, and re-layouts  0.75 us (1%)
    ppermute x4, starting transfers between devices, swap(): return lambda x: lax.ppermute(x, axes, pairs)  17.9 us
    all_to_all x1, starting transfers between devices, local(): lax.all_to_all(outbox.reshape(lat_n * lon_n, CAP, NT * LEV), axes, split_...  8.23 us
    pallas_call x1, Pallas kernels, store_cells(): pl.pallas_call(store_kernel, in_specs=[vmem()], out_specs=vmem(), out_sha...  5.58 us
    all_to_all x1, waiting for transfers between devices, local(): lax.all_to_all(outbox.reshape(lat_n * lon_n, CAP, NT * LEV), axes, split_...  5.45 us
    pallas_call x1, Pallas kernels, load_cells(): pl.pallas_call(load_kernel, in_specs=[vmem()] * 5, out_specs=vmem(), out_...  4.4 us
    pallas_call x1, Pallas kernels, inner_steps(): pl.pallas_call(inner_kernel, in_specs=[vmem()] * 2, out_specs=[vmem()] *...  4.18 us
    pallas_call x1, Pallas kernels, outer_steps(): pl.pallas_call(outer_kernel, in_specs=[vmem()] * 4 + [smem, smem], out_sp...  3.56 us
    pallas_call x1, Pallas kernels, pack_rows(): pl.pallas_call(body, grid=(1,), in_specs=[tile(x.shape[0], t) for x in (q...  1.63 us
  transfers between devices with their start and end apart: 5, of which 2 were waited for; matrix products, arithmetic and copies ran while one was open for 0% of the time, Pallas kernels for 26%

profile of v4, /device:TPU:1, one launch (start us, length us, event | category | flops | bytes accessed | tf_op | source)
XLA Modules:
  0.0 54.6 jit_solution(15275005435670970591)
XLA Ops:
  0.6 0.0 copy-start.4
  0.6 0.7 %copy-done.4 = f32[32,128]{1,0:T(8,128)S(1)} copy-done((f32[32,128]{1,0:T(8,128)S(1)}, f32[32,128]{1,0:T(8,128)}, u32[]{:S(2)}) %copy-start.4) | copy-done | bytes 16408
  1.3 1.6 %pack_rows.1 = (f32[23,32,128]{2,1,0:T(8,128)S(1)}, f32[23,32,128]{2,1,0:T(8,128)S(1)}) custom-call(f32[128,32,128]{2,1,0:T(8,128)} %bitcast.11, f32[128,32,128]{2,1,0:T(8,128)} %bitcast.12, f32[32,32,128]{2,1,0:T(8,128)} %refs_3_.1, f32[32,32,128]{2,1,0:T(8,128)} %refs_3_.1, f32[32,32,128]{2,1,0:T(8,128)} %refs_5_.1, f32[32,32,128]{2,1,0:T(8,128)} %refs_5_.1, ...), custom_call_target="tpu_custom_call" | custom-call | tf_op jit(solution)/shard_map/pack_rows/pallas_call | solution.py:106
  3.0 0.0 copy-start
  3.0 0.0 copy-start.1
  3.0 0.0 copy-start.2
  3.0 0.0 copy-start.3
  3.0 1.5 %collective-permute-start = (f32[23,32,128]{2,1,0:T(8,128)S(1)}, f32[23,32,128]{2,1,0:T(8,128)S(1)}, u32[]{:S(2)}, u32[]{:S(2)}) collective-permute-start(f32[23,32,128]{2,1,0:T(8,128)S(1)} %get-tuple-element.19), channel_id=1, source_target_pairs={{0,32},{1,33},{2,34},{3,35},{4,36},{5,37},{6,38},{7,39},{8,40},{9,... | collective-permute-start | bytes 1130504 | tf_op jit(solution)/shard_map/ppermute | solution.py:492
  4.5 3.8 %collective-permute-start.1 = (f32[23,32,128]{2,1,0:T(8,128)S(1)}, f32[23,32,128]{2,1,0:T(8,128)S(1)}, u32[]{:S(2)}, u32[]{:S(2)}) collective-permute-start(f32[23,32,128]{2,1,0:T(8,128)S(1)} %get-tuple-element.20), channel_id=1, source_target_pairs={{32,64},{33,65},{34,66},{35,67},{36,68},{37,69},{38,70},{39,71},{4... | collective-permute-start | bytes 1130504 | tf_op jit(solution)/shard_map/ppermute | solution.py:492
  8.3 0.0 copy-done
  8.3 0.0 copy-done.1
  8.4 0.0 copy-done.2
  8.4 0.0 copy-done.3
  8.4 0.0 copy-start.5
  8.4 4.4 %load_cells.1.big_in = f32[37728,128]{1,0:T(8,128)S(1)} custom-call(f32[4096,128]{1,0:T(8,128)S(1)} %bitcast.13, f32[1024,128]{1,0:T(8,128)S(1)} %bitcast.14, f32[1024,128]{1,0:T(8,128)S(1)} %bitcast.15, s32[1024,128]{1,0:T(8,128)S(1)} %bitcast.16, f32[32,128]{1,0:T(8,128)S(1)} %copy-done.4), custom_call_target="tpu_custom_call" | custom-call | bytes 16000000 | tf_op jit(solution)/shard_map/load_cells/pallas_call | solution.py:163
  12.8 0.0 copy-start.6
  12.8 0.0 collective-permute-done.in_p
  12.8 0.8 %collective-permute-done.1.in_q = f32[23,32,128]{2,1,0:T(8,128)S(1)} collective-permute-done((f32[23,32,128]{2,1,0:T(8,128)S(1)}, f32[23,32,128]{2,1,0:T(8,128)S(1)}, u32[]{:S(2)}, u32[]{:S(2)}) %collective-permute-start.1) | collective-permute-done | bytes 376864 | tf_op jit(solution)/shard_map/ppermute | solution.py:492
  13.6 0.5 ghost_rows.1
  14.2 3.7 %collective-permute-start.2 = (f32[288,128]{1,0:T(8,128)S(1)}, f32[288,128]{1,0:T(8,128)S(1)}, u32[]{:S(2)}, u32[]{:S(2)}) collective-permute-start(f32[288,128]{1,0:T(8,128)S(1)} %get-tuple-element.24), channel_id=1, source_target_pairs={{0,1},{1,0},{2,3},{3,2},{4,5},{5,4},{6,7},{7,6},{8,9},{9,8},{10,11... | collective-permute-start | bytes 442376 | tf_op jit(solution)/shard_map/ppermute | solution.py:492
  17.9 8.8 %collective-permute-start.3 = (f32[288,128]{1,0:T(8,128)S(1)}, f32[288,128]{1,0:T(8,128)S(1)}, u32[]{:S(2)}, u32[]{:S(2)}) collective-permute-start(f32[288,128]{1,0:T(8,128)S(1)} %get-tuple-element.25), channel_id=1, source_target_pairs={{0,31},{1,2},{2,1},{3,4},{4,3},{5,6},{6,5},{7,8},{8,7},{9,10},{10,... | collective-permute-start | bytes 442376 | tf_op jit(solution)/shard_map/ppermute | solution.py:492
  26.7 0.0 copy-done.5
  26.7 4.2 %inner_steps.1 = (f32[37728,128]{1,0:T(8,128)S(1)}, f32[4096,128]{1,0:T(8,128)S(1)}, s32[1,256]{1,0:T(1,128)S(1)}) custom-call(f32[37728,128]{1,0:T(8,128)S(1)} %get-tuple-element.21.big_in, s32[1,256]{1,0:T(1,128)S(1)} %bitcast.18), custom_call_target="tpu_custom_call", output_to_operand_aliasing={{0}: (0, {})} | custom-call | flops 40000000 | bytes 20000000 | tf_op jit(solution)/shard_map/inner_steps/pallas_call | solution.py:363
  30.9 0.0 collective-permute-done.2.in_r
  30.9 0.0 collective-permute-done.3.in_s
  31.0 0.0 copy-done.6
  31.0 3.6 %outer_steps.1 = (f32[37728,128]{1,0:T(8,128)S(1)}, f32[4096,128]{1,0:T(8,128)S(1)}, f32[512,128]{1,0:T(8,128)}) custom-call(f32[37728,128]{1,0:T(8,128)S(1)} %get-tuple-element.22.big_in, f32[4096,128]{1,0:T(8,128)S(1)} %get-tuple-element.23.after_in, f32[288,128]{1,0:T(8,128)S(1)} %collective-permute-done.2.in_r, ...), custom_call_target="tpu_custom_call", output_to_operand_aliasing={{0}: (0, {}), {1}: (1, {})} | custom-call | tf_op jit(solution)/shard_map/outer_steps/pallas_call | solution.py:425
  34.5 8.2 %all-to-all-start = ((f32[128,4,128]{2,1,0:T(4,128)}), f32[128,4,128]{2,1,0:T(4,128)S(1)}, u32[]{:S(2)}, u32[]{:S(2)}) async-start(f32[128,4,128]{2,1,0:T(4,128)} %bitcast.8), calls=%async_computation | async-start | bytes 524288 | tf_op jit(solution)/shard_map/all_to_all | solution.py:511
  42.8 5.6 %store_cells.1 = f32[4096,128]{1,0:T(8,128)} custom-call(f32[4096,128]{1,0:T(8,128)S(1)} %get-tuple-element.27.after), custom_call_target="tpu_custom_call" | custom-call | bytes 8000000 | tf_op jit(solution)/shard_map/store_cells/pallas_call | solution.py:448
  48.3 5.4 %all-to-all-done = f32[128,4,128]{2,1,0:T(4,128)S(1)} async-done(((f32[128,4,128]{2,1,0:T(4,128)}), f32[128,4,128]{2,1,0:T(4,128)S(1)}, u32[]{:S(2)}, u32[]{:S(2)}) %all-to-all-start) | async-done | bytes 262176 | tf_op jit(solution)/shard_map/all_to_all | solution.py:511
  53.8 0.8 %unpack_arrivals.1 = (f32[512,128]{1,0:T(8,128)}, s32[1,128]{1,0:T(1,128)}) custom-call(f32[512,128]{1,0:T(8,128)S(1)} %bitcast.17), custom_call_target="tpu_custom_call" | custom-call | tf_op jit(solution)/shard_map/unpack_arrivals/pallas_call | solution.py:473
  (1 shorter events, 0.0 us)
Async XLA Ops:
  0.6 0.7 %copy-start.4 = (f32[32,128]{1,0:T(8,128)S(1)}, f32[32,128]{1,0:T(8,128)}, u32[]{:S(2)}) copy-start(f32[32,128]{1,0:T(8,128)} %refs_8_.1) | copy-start | bytes 49156
  3.0 5.3 %copy-start = (f32[4,32,32,128]{3,2,1,0:T(8,128)S(1)}, f32[4,32,32,128]{3,2,1,0:T(8,128)}, u32[]{:S(2)}) copy-start(f32[4,32,32,128]{3,2,1,0:T(8,128)} %param.7) | copy-start | bytes 6291460
  3.0 5.3 %copy-start.1 = (f32[32,32,128]{2,1,0:T(8,128)S(1)}, f32[32,32,128]{2,1,0:T(8,128)}, u32[]{:S(2)}) copy-start(f32[32,32,128]{2,1,0:T(8,128)} %refs_3_.1) | copy-start | bytes 1572868
  3.0 5.3 %copy-start.2 = (f32[32,32,128]{2,1,0:T(8,128)S(1)}, f32[32,32,128]{2,1,0:T(8,128)}, u32[]{:S(2)}) copy-start(f32[32,32,128]{2,1,0:T(8,128)} %refs_5_.1) | copy-start | bytes 1572868
  3.0 5.3 %copy-start.3 = (s32[32,32,128]{2,1,0:T(8,128)S(1)}, s32[32,32,128]{2,1,0:T(8,128)}, u32[]{:S(2)}) copy-start(s32[32,32,128]{2,1,0:T(8,128)} %refs_7_.1) | copy-start | bytes 1572868
  3.0 9.8 %collective-permute-start = (f32[23,32,128]{2,1,0:T(8,128)S(1)}, f32[23,32,128]{2,1,0:T(8,128)S(1)}, u32[]{:S(2)}, u32[]{:S(2)}) collective-permute-start(f32[23,32,128]{2,1,0:T(8,128)S(1)} %get-tuple-element.19), channel_id=1, source_target_pairs={{0,32},{1,33},{2,34},{3,35},{4,36},{5,37},{6,38},{7,39},{8,40},{9,... | collective-permute-start | bytes 1130504 | tf_op jit(solution)/shard_map/ppermute | solution.py:492
  4.5 9.1 %collective-permute-start.1 = (f32[23,32,128]{2,1,0:T(8,128)S(1)}, f32[23,32,128]{2,1,0:T(8,128)S(1)}, u32[]{:S(2)}, u32[]{:S(2)}) collective-permute-start(f32[23,32,128]{2,1,0:T(8,128)S(1)} %get-tuple-element.20), channel_id=1, source_target_pairs={{32,64},{33,65},{34,66},{35,67},{36,68},{37,69},{38,70},{39,71},{4... | collective-permute-start | bytes 1130504 | tf_op jit(solution)/shard_map/ppermute | solution.py:492
  8.4 18.4 %copy-start.5 = (s32[256,1]{0,1:T(1,128)S(1)}, s32[256,1]{0,1:T(1,128)}, u32[]{:S(2)}) copy-start(s32[256,1]{0,1:T(1,128)} %param.13) | copy-start | bytes 3076
  12.8 18.2 %copy-start.6 = (s32[256]{0:T(256)S(1)}, s32[256]{0:T(256)}, u32[]{:S(2)}) copy-start(s32[256]{0:T(256)} %cell.1) | copy-start | bytes 3076
  14.2 16.8 %collective-permute-start.2 = (f32[288,128]{1,0:T(8,128)S(1)}, f32[288,128]{1,0:T(8,128)S(1)}, u32[]{:S(2)}, u32[]{:S(2)}) collective-permute-start(f32[288,128]{1,0:T(8,128)S(1)} %get-tuple-element.24), channel_id=1, source_target_pairs={{0,1},{1,0},{2,3},{3,2},{4,5},{5,4},{6,7},{7,6},{8,9},{9,8},{10,11... | collective-permute-start | bytes 442376 | tf_op jit(solution)/shard_map/ppermute | solution.py:492
  17.9 13.0 %collective-permute-start.3 = (f32[288,128]{1,0:T(8,128)S(1)}, f32[288,128]{1,0:T(8,128)S(1)}, u32[]{:S(2)}, u32[]{:S(2)}) collective-permute-start(f32[288,128]{1,0:T(8,128)S(1)} %get-tuple-element.25), channel_id=1, source_target_pairs={{0,31},{1,2},{2,1},{3,4},{4,3},{5,6},{6,5},{7,8},{8,7},{9,10},{10,... | collective-permute-start | bytes 442376 | tf_op jit(solution)/shard_map/ppermute | solution.py:492
  34.5 19.3 %all-to-all-start = ((f32[128,4,128]{2,1,0:T(4,128)}), f32[128,4,128]{2,1,0:T(4,128)S(1)}, u32[]{:S(2)}, u32[]{:S(2)}) async-start(f32[128,4,128]{2,1,0:T(4,128)} %bitcast.8), calls=%async_computation | async-start | bytes 524288 | tf_op jit(solution)/shard_map/all_to_all | solution.py:511
